TPU v7x, 256 devices: a whole 4x4x8 slice. The times are simulated.
256 devices in a mesh: grp: 32 (over y, x, core), own: 8 (over z).
Axes of the slice: x: 4, y: 4, z: 8, core: 2. Of those that a mesh axis runs over, the one named last changes fastest.
Arguments:
- embeddings: bfloat16 [2048, 32, 1024], P(('grp', 'own')), may hold values from -16 to 16
- cluster_ids: int32 [2048, 32], P(('grp', 'own')), may hold values from 0 to 3
- owners: int32 [2048, 1], P(('grp', 'own')), may hold values from 0 to 7; in each aligned block of 8 rows (0 to 7, 8 to 15, ...) at most 2 rows name the same one
- pattern: int32 [32, 32], replicated, may hold values 0 or 1
Outputs:
- best: float32 [2048, 32], P(('grp', 'own'))
Inputs may be any that keep to these rules, and one draw needn't show every extreme that they name: `owners`: A device sends at most 2 tiles to one owner; some device sends exactly 2 tiles to one owner.
All inputs are finite; a program needn't handle non-finite values.
Results may differ from a plain program's by a relative error of at most 0.00057.
Values may be sent and summed in bfloat16 or wider, within the bound.
No kernel may reach another device: no remote copies, remote signals or barrier semaphores. Data moves between devices by JAX's collectives and lax.ppermute only.
A program may use at most 64 MiB of HBM per device.

v0:
```python
import functools

import jax
import jax.numpy as jnp
from jax import lax
from jax.experimental import pallas as pl
from jax.experimental.pallas import tpu as pltpu
from jax.sharding import PartitionSpec as P


TILE = 32
GROUP = 8
ROWS = TILE * GROUP
CHUNKS = (4 * ROWS, 5 * ROWS)

TREE = (
    ((0, 0), (1, 0)),
    ((0, 0), (-1, 0)),
    ((0, 0), (0, 1)),
    ((0, 0), (0, -1)),
    ((0, 1), (1, 0)),
    ((0, -1), (-1, 0)),
    ((-1, 0), (0, 1)),
    ((1, 0), (0, -1)),
    ((1, 0), (1, 0)),
    ((-1, -1), (-1, 0)),
    ((0, 1), (0, 1)),
    ((1, -1), (0, -1)),
    ((1, 1), (1, 0)),
    ((-1, 1), (0, 1)),
    ((2, 3), (0, -1)),
)
SIDE = 4
OWNERS = 8
CLUSTERS = 4


def wrap(node):
    return (node[0] % SIDE, node[1] % SIDE)


def plane_pairs(dx, dy, flip):
    pairs = []
    for y in range(SIDE):
        for x in range(SIDE):
            for core in range(2):
                source = (y * SIDE + x) * 2 + core
                dest = (((y + dy) % SIDE) * SIDE + (x + dx) % SIDE) * 2 + (core ^ flip)
                pairs.append((source, dest))
    return pairs


def in_plane(value, dx, dy):
    return lax.ppermute(value, "grp", plane_pairs(dx, dy, 0))


def other_core(value):
    return lax.ppermute(value, "grp", plane_pairs(0, 0, 1))


def along(value, step, count):
    return lax.ppermute(value, "own", [(i, (i + step) % count) for i in range(count)])


def unit_rows(values):
    wide = values.astype(jnp.float32)
    return (wide * lax.rsqrt(jnp.sum(wide * wide, axis=-1, keepdims=True) + 1e-06)).astype(
        jnp.bfloat16
    )


def compare_kernel(queries, keys, where_ref, pattern_ref, *refs):
    n_ops = max([h for _, h, _ in queries] + [k[0] for k in keys]) + 1
    arrays = refs[:n_ops]
    out_ref, q_raw, k_raw, q_col, k_col, acc, spread, meta, own_vec = refs[n_ops : n_ops + 9]
    own_s, k_base, q_next, k_next, q_order, q_own_s, k_order, sems = refs[n_ops + 9 : n_ops + 17]
    q_rows, q_names, found_rows = refs[n_ops + 17 :]
    n_q, n_k = len(queries), len(keys)
    k_tiles, blocks = n_k * GROUP, n_q + OWNERS
    small, large = (chunk // TILE for chunk in CHUNKS)
    half = ROWS // 2
    group, depth = where_ref[0], where_ref[1]
    chip_y, chip_x, core = group // (2 * SIDE), (group // 2) % SIDE, group % 2

    for i in range(n_q + n_k):
        if i < n_q:
            low, high, _ = queries[i]
            row = ROWS if low == high else half
        else:
            high, row = keys[i - n_q][0], ROWS
        pltpu.make_async_copy(
            arrays[high].at[pl.ds(row, 8), pl.ds(0, ROWS)], meta.at[i], sems.at[0]
        ).start()
    for i in range(n_q):
        low, high, _ = queries[i]
        if low == high:
            parts = [(low, i * ROWS, ROWS)]
        else:
            parts = [(low, i * ROWS, half), (high, i * ROWS + half, half)]
        for ref, to, rows in parts:
            pltpu.make_async_copy(
                arrays[ref].at[pl.ds(0, rows)], q_raw.at[pl.ds(to, rows)], sems.at[1]
            ).start()
    for i in range(n_k):
        pltpu.make_async_copy(
            arrays[keys[i][0]].at[pl.ds(0, ROWS)], k_raw.at[pl.ds(i * ROWS, ROWS)], sems.at[2]
        ).start()
    pltpu.make_async_copy(meta, meta, sems.at[0]).wait()
    for i in range(n_q + n_k):
        own_vec[i : i + 1, :] = meta[i].astype(jnp.float32)[1:2, :].astype(jnp.int32)
    to_scalar = pltpu.make_async_copy(own_vec, own_s, sems.at[0])
    to_scalar.start()

    def column(row):
        return jnp.transpose(jnp.broadcast_to(row, (128, ROWS)))

    def label(i):
        info = meta[i].astype(jnp.float32)
        return info[1:2, :] * CLUSTERS + info[0:1, :]

    for i in range(n_q):
        q_col[i * ROWS : (i + 1) * ROWS, :] = column(label(i))
    q_col[n_q * ROWS :, :] = jnp.full((TILE, 128), -3.0, jnp.float32)
    for i in range(n_k):
        _, dx, dy, flip = keys[i]
        source = (((chip_y - dy) % SIDE) * SIDE + (chip_x - dx) % SIDE) * 2 + (core + flip) % 2
        allowed = pattern_ref[group, source] > 0
        k_col[i * ROWS : (i + 1) * ROWS, :] = column(jnp.where(allowed, label(n_q + i), -1.0))
    found_rows[...] = jnp.full_like(found_rows, -1.0)
    to_scalar.wait()

    for o in range(OWNERS + 1):
        q_next[o] = 0
        k_next[o] = 0

    def count(i, table):
        for j in range(GROUP):
            o = own_s[i, j * TILE]
            table[o] = table[o] + 1

    def count_q(i, carry):
        count(i, q_next)
        return carry

    def count_k(i, carry):
        count(i, k_next)
        return carry

    lax.fori_loop(0, n_q, count_q, 0)
    lax.fori_loop(n_q, n_q + n_k, count_k, 0)
    q_total, k_total = jnp.int32(0), jnp.int32(0)
    for o in range(OWNERS + 1):
        q_here, k_here = q_next[o], k_next[o]
        q_next[o], k_next[o] = q_total, k_total
        k_base[o] = k_total
        q_total = q_total + (q_here + GROUP - 1) // GROUP * GROUP
        k_total = k_total + k_here

    def no_tile(t, carry):
        q_order[t] = n_q * GROUP
        return carry

    lax.fori_loop(0, blocks * GROUP, no_tile, 0, unroll=8)

    def put_q(i, carry):
        for j in range(GROUP):
            o = own_s[i, j * TILE]
            to = q_next[o]
            q_next[o] = to + 1
            q_order[to] = i * GROUP + j
            q_own_s[to // GROUP] = o
        return carry

    def put_k(i, carry):
        for j in range(GROUP):
            o = own_s[n_q + i, j * TILE]
            to = k_next[o]
            k_next[o] = to + 1
            k_order[to] = i * GROUP + j
        return carry

    lax.fori_loop(0, n_q, put_q, 0)
    lax.fori_loop(0, n_k, put_k, 0)

    def tile_rows(t):
        return pl.ds(pl.multiple_of(t * TILE, TILE), TILE)

    inside = lax.broadcasted_iota(jnp.int32, (TILE, 128), 0)

    def names(t, other):
        return inside + jnp.where(t < GROUP, t * TILE, other)

    for b in range(blocks):
        tiles = [q_order[b * GROUP + j] for j in range(GROUP)]
        col = jnp.concatenate([q_col[tile_rows(t), :] for t in tiles], axis=0)
        q_rows[b] = jnp.transpose(col)[0:1, :]
        name = jnp.concatenate([names(t, -(1 << 20)) for t in tiles], axis=0)
        q_names[b] = jnp.transpose(name.astype(jnp.float32))[0:1, :].astype(jnp.int32)
    pltpu.make_async_copy(q_raw, q_raw, sems.at[1]).wait()
    pltpu.make_async_copy(k_raw, k_raw, sems.at[2]).wait()

    def block_step(b, carry):
        owner = q_own_s[b]
        lo = k_base[owner]
        q_row, q_name = q_rows[b], q_names[b]
        acc[...] = jnp.full_like(acc, -1.0)
        q_at = [jnp.minimum(q_order[b * GROUP + j], n_q * GROUP - 1) for j in range(GROUP)]

        here = k_base[owner + 1] - lo

        def chunk_step(per, m):
            tiles = [
                k_order[jnp.minimum(lo + m * per + i, k_tiles - 1)] for i in range(per)
            ]
            block = jnp.concatenate([q_raw[tile_rows(t), :] for t in q_at], axis=0)
            scores = lax.dot_general(
                jnp.concatenate([k_raw[tile_rows(t), :] for t in tiles], axis=0), block,
                (((1,), (1,)), ((), ())), preferred_element_type=jnp.float32,
            )
            col = jnp.concatenate([k_col[tile_rows(t), :] for t in tiles], axis=0)
            name = jnp.concatenate([names(t, -(1 << 21)) for t in tiles], axis=0)
            for h in range(ROWS // 128):
                lanes = slice(h * 128, (h + 1) * 128)
                match = (col == q_row[:, lanes]) & (name != q_name[:, lanes])
                found = jnp.where(match, scores[:, lanes], -1.0)
                found = jnp.max(found.reshape(per * TILE // 8, 8, 128), axis=0)
                acc[:, lanes] = jnp.maximum(acc[:, lanes], found)

        def large_step(m, inner):
            chunk_step(large, m)
            return inner

        fits = here <= small

        @pl.when(fits)
        def _():
            chunk_step(small, 0)

        lax.fori_loop(0, jnp.where(fits, 0, (here + large - 1) // large), large_step, 0)
        found_rows[b] = jnp.max(acc[...], axis=0, keepdims=True)
        return carry

    lax.fori_loop(0, q_total // GROUP, block_step, 0)
    for b in range(blocks):
        done = column(found_rows[b])
        for j in range(GROUP):
            spread[tile_rows(q_order[b * GROUP + j]), :] = done[j * TILE : (j + 1) * TILE, :]
    for s in range(n_q):
        to = (depth - queries[s][2] + 2 * n_q) % n_q
        out_ref[to] = jnp.transpose(spread[s * ROWS : (s + 1) * ROWS, :])[0:1, :]


def compare(where, pattern, arrays, queries, keys):
    n_q, n_k = len(queries), len(keys)
    width = arrays[0].shape[1]
    blocks = n_q + OWNERS
    smem = pl.BlockSpec(memory_space=pltpu.SMEM)
    anywhere = pl.BlockSpec(memory_space=pl.ANY)
    slots = -(-(n_q + n_k) // 8) * 8
    return pl.pallas_call(
        functools.partial(compare_kernel, queries, keys),
        out_shape=jax.ShapeDtypeStruct((n_q, 1, ROWS), jnp.float32),
        in_specs=[smem] * 2 + [anywhere] * len(arrays),
        out_specs=pl.BlockSpec(memory_space=pltpu.VMEM),
        scratch_shapes=[
            pltpu.VMEM((n_q * ROWS, width), jnp.bfloat16),
            pltpu.VMEM((n_k * ROWS, width), jnp.bfloat16),
            pltpu.VMEM((n_q * ROWS + TILE, 128), jnp.float32),
            pltpu.VMEM((n_k * ROWS, 128), jnp.float32),
            pltpu.VMEM((8, ROWS), jnp.float32),
            pltpu.VMEM((n_q * ROWS + TILE, 128), jnp.float32),
            pltpu.VMEM((n_q + n_k, 8, ROWS), jnp.bfloat16),
            pltpu.VMEM((slots, ROWS), jnp.int32),
            pltpu.SMEM((slots, ROWS), jnp.int32),
            pltpu.SMEM((OWNERS + 1,), jnp.int32),
            pltpu.SMEM((OWNERS + 1,), jnp.int32),
            pltpu.SMEM((OWNERS + 1,), jnp.int32),
            pltpu.SMEM((blocks * GROUP,), jnp.int32),
            pltpu.SMEM((blocks,), jnp.int32),
            pltpu.SMEM((n_k * GROUP,), jnp.int32),
            pltpu.SemaphoreType.DMA((3,)),
            pltpu.VMEM((blocks, 1, ROWS), jnp.float32),
            pltpu.VMEM((blocks, 1, ROWS), jnp.int32),
            pltpu.VMEM((blocks, 1, ROWS), jnp.float32),
        ],
        cost_estimate=pl.CostEstimate(
            flops=2 * n_q * n_k * ROWS * ROWS * width // 4,
            bytes_accessed=(n_q + n_k) * ROWS * width * 2,
            transcendentals=0,
        ),
        name="compare",
    )(where, pattern, *arrays)


def search(embeddings, cluster_ids, owners, pattern):
    n_own = lax.axis_size("own")
    tiles_here, tile_rows, width = embeddings.shape
    where = jnp.stack([lax.axis_index("grp"), lax.axis_index("own")]).astype(jnp.int32)

    labels = jnp.stack([cluster_ids, jnp.broadcast_to(owners, cluster_ids.shape)])
    labels = labels.reshape(2, ROWS).astype(jnp.bfloat16)
    labels = jnp.pad(labels, ((0, 6), (0, width - ROWS)))
    shard = jnp.concatenate([unit_rows(embeddings).reshape(ROWS, width), labels], axis=0)

    up, down = [shard], [shard]
    arrays = [shard]
    queries = [(0, 0, 0)]
    for hop in range(1, n_own // 2):
        up.append(along(up[-1], 1, n_own))
        down.append(along(down[-1], -1, n_own))
        at = len(arrays)
        queries += [(at, at, hop), (at + 1, at + 1, -hop)]
        arrays += [up[-1], down[-1]]
    far_low = along(up[-1][: ROWS // 2], 1, n_own)
    far_high = along(down[-1][ROWS // 2 :], -1, n_own)
    queries.append((len(arrays), len(arrays) + 1, n_own // 2))
    arrays += [far_low, far_high]

    held = {(0, 0): shard}
    keys = [(0, 0, 0, 0), (len(arrays), 0, 0, 1)]
    arrays.append(other_core(shard))
    for source, (dx, dy) in TREE:
        node = wrap((source[0] + dx, source[1] + dy))
        held[node] = in_plane(held[wrap(source)], dx, dy)
        keys += [(len(arrays), *node, 0), (len(arrays) + 1, *node, 1)]
        arrays += [held[node], other_core(held[node])]
    best = compare(where, pattern, arrays, queries, keys)

    returned = lax.all_to_all(best, "own", split_axis=0, concat_axis=0, tiled=True)
    return jnp.max(returned, axis=0).reshape(tiles_here, tile_rows)


def solution(mesh):
    placed = (P(("grp", "own"), None, None), P(("grp", "own"), None), P(("grp", "own"), None), P())
    return jax.shard_map(
        search, mesh=mesh, in_specs=placed, out_specs=P(("grp", "own"), None), check_vma=False
    )
```

profile of v0, /device:TPU:32, one launch (start us, length us, event | category | flops | bytes accessed | tf_op | source)
XLA Modules:
  0.0 142.3 jit_solution(18259406142015786816)
XLA Ops:
  0.0 1.3 fusion
  1.3 0.2 fusion.1
  1.5 0.5 copy-done.32
  2.3 3.1 %collective-permute-start.15 = (bf16[264,1024]{1,0:T(8,128)(2,1)S(1)}, bf16[264,1024]{1,0:T(8,128)(2,1)S(1)}, u32[]{:S(2)}, u32[]{:S(2)}) collective-permute-start(bf16[264,1024]{1,0:T(8,128)(2,1)S(1)} %pad_maximum_fusion.refs_0_), channel_id=1, source_target_pairs={{0,192},{8,200},{16,208},{24,216},{32,224},{40,232},{48,240},{56,2... | collective-permute-start | bytes 1622024 | tf_op jit(solution)/shard_map/ppermute | solution.py:54
  5.4 1.5 %collective-permute-start.9 = (bf16[264,1024]{1,0:T(8,128)(2,1)S(1)}, bf16[264,1024]{1,0:T(8,128)(2,1)S(1)}, u32[]{:S(2)}, u32[]{:S(2)}) collective-permute-start(bf16[264,1024]{1,0:T(8,128)(2,1)S(1)} %pad_maximum_fusion.refs_0_), channel_id=1, source_target_pairs={{0,16},{8,24},{16,32},{24,40},{32,48},{40,56},{48,0},{56,8},{64,80... | collective-permute-start | bytes 1622024 | tf_op jit(solution)/shard_map/ppermute | solution.py:54
  6.9 1.7 %collective-permute-start.11 = (bf16[264,1024]{1,0:T(8,128)(2,1)S(1)}, bf16[264,1024]{1,0:T(8,128)(2,1)S(1)}, u32[]{:S(2)}, u32[]{:S(2)}) collective-permute-start(bf16[264,1024]{1,0:T(8,128)(2,1)S(1)} %pad_maximum_fusion.refs_0_), channel_id=1, source_target_pairs={{0,48},{8,56},{16,0},{24,8},{32,16},{40,24},{48,32},{56,40},{64,11... | collective-permute-start | bytes 1622024 | tf_op jit(solution)/shard_map/ppermute | solution.py:54
  8.6 0.8 collective-permute-start.1
  9.4 7.5 %collective-permute-done.15.refs_16_ = bf16[264,1024]{1,0:T(8,128)(2,1)S(1)} collective-permute-done((bf16[264,1024]{1,0:T(8,128)(2,1)S(1)}, bf16[264,1024]{1,0:T(8,128)(2,1)S(1)}, u32[]{:S(2)}, u32[]{:S(2)}) %collective-permute-start.15) | collective-permute-done | bytes 540704 | tf_op jit(solution)/shard_map/ppermute | solution.py:54
  16.9 1.9 %collective-permute-start = (bf16[264,1024]{1,0:T(8,128)(2,1)S(1)}, bf16[264,1024]{1,0:T(8,128)(2,1)S(1)}, u32[]{:S(2)}, u32[]{:S(2)}) collective-permute-start(bf16[264,1024]{1,0:T(8,128)(2,1)S(1)} %pad_maximum_fusion.refs_0_), channel_id=1, source_target_pairs={{0,1},{1,2},{2,3},{3,4},{4,5},{5,6},{6,7},{7,0},{8,9},{9,10},{10,1... | collective-permute-start | bytes 1622024 | tf_op jit(solution)/shard_map/ppermute | solution.py:62
  18.8 1.5 %collective-permute-done.9.refs_10_ = bf16[264,1024]{1,0:T(8,128)(2,1)S(1)} collective-permute-done((bf16[264,1024]{1,0:T(8,128)(2,1)S(1)}, bf16[264,1024]{1,0:T(8,128)(2,1)S(1)}, u32[]{:S(2)}, u32[]{:S(2)}) %collective-permute-start.9) | collective-permute-done | bytes 540704 | tf_op jit(solution)/shard_map/ppermute | solution.py:54
  20.3 1.2 collective-permute-done.13.refs_14_
  21.5 1.7 %collective-permute-start.19 = (bf16[264,1024]{1,0:T(8,128)(2,1)S(1)}, bf16[264,1024]{1,0:T(8,128)(2,1)S(1)}, u32[]{:S(2)}, u32[]{:S(2)}) collective-permute-start(bf16[264,1024]{1,0:T(8,128)(2,1)S(1)} %collective-permute-done.15.refs_16_), channel_id=1, source_target_pairs={{0,48},{8,56},{16,0},{24,8},{32,16},{40,24},{48,32},{56,40},{64,11... | collective-permute-start | bytes 1622024 | tf_op jit(solution)/shard_map/ppermute | solution.py:54
  23.3 2.1 %collective-permute-start.23 = (bf16[264,1024]{1,0:T(8,128)(2,1)S(1)}, bf16[264,1024]{1,0:T(8,128)(2,1)S(1)}, u32[]{:S(2)}, u32[]{:S(2)}) collective-permute-start(bf16[264,1024]{1,0:T(8,128)(2,1)S(1)} %collective-permute-done.9.refs_10_), channel_id=1, source_target_pairs={{0,192},{8,200},{16,208},{24,216},{32,224},{40,232},{48,240},{56,2... | collective-permute-start | bytes 1622024 | tf_op jit(solution)/shard_map/ppermute | solution.py:54
  25.4 4.7 %collective-permute-done.refs_1_ = bf16[264,1024]{1,0:T(8,128)(2,1)S(1)} collective-permute-done((bf16[264,1024]{1,0:T(8,128)(2,1)S(1)}, bf16[264,1024]{1,0:T(8,128)(2,1)S(1)}, u32[]{:S(2)}, u32[]{:S(2)}) %collective-permute-start) | collective-permute-done | bytes 540704 | tf_op jit(solution)/shard_map/ppermute | solution.py:62
  30.1 1.0 collective-permute-start.21
  31.1 1.5 %collective-permute-start.25 = (bf16[264,1024]{1,0:T(8,128)(2,1)S(1)}, bf16[264,1024]{1,0:T(8,128)(2,1)S(1)}, u32[]{:S(2)}, u32[]{:S(2)}) collective-permute-start(bf16[264,1024]{1,0:T(8,128)(2,1)S(1)} %collective-permute-done.9.refs_10_), channel_id=1, source_target_pairs={{0,16},{8,24},{16,32},{24,40},{32,48},{40,56},{48,0},{56,8},{64,80... | collective-permute-start | bytes 1622024 | tf_op jit(solution)/shard_map/ppermute | solution.py:54
  32.6 2.4 %collective-permute-done.19.refs_20_ = bf16[264,1024]{1,0:T(8,128)(2,1)S(1)} collective-permute-done((bf16[264,1024]{1,0:T(8,128)(2,1)S(1)}, bf16[264,1024]{1,0:T(8,128)(2,1)S(1)}, u32[]{:S(2)}, u32[]{:S(2)}) %collective-permute-start.19) | collective-permute-done | bytes 540704 | tf_op jit(solution)/shard_map/ppermute | solution.py:54
  35.0 2.2 %collective-permute-done.23.refs_24_ = bf16[264,1024]{1,0:T(8,128)(2,1)S(1)} collective-permute-done((bf16[264,1024]{1,0:T(8,128)(2,1)S(1)}, bf16[264,1024]{1,0:T(8,128)(2,1)S(1)}, u32[]{:S(2)}, u32[]{:S(2)}) %collective-permute-start.23) | collective-permute-done | bytes 540704 | tf_op jit(solution)/shard_map/ppermute | solution.py:54
  37.2 1.2 collective-permute-start.3
  38.4 3.3 %collective-permute-done.17.refs_18_ = bf16[264,1024]{1,0:T(8,128)(2,1)S(1)} collective-permute-done((bf16[264,1024]{1,0:T(8,128)(2,1)S(1)}, bf16[264,1024]{1,0:T(8,128)(2,1)S(1)}, u32[]{:S(2)}, u32[]{:S(2)}) %collective-permute-start.17) | collective-permute-done | bytes 540704 | tf_op jit(solution)/shard_map/ppermute | solution.py:54
  41.8 1.9 %collective-permute-start.2 = (bf16[264,1024]{1,0:T(8,128)(2,1)S(1)}, bf16[264,1024]{1,0:T(8,128)(2,1)S(1)}, u32[]{:S(2)}, u32[]{:S(2)}) collective-permute-start(bf16[264,1024]{1,0:T(8,128)(2,1)S(1)} %collective-permute-done.refs_1_), channel_id=1, source_target_pairs={{0,1},{1,2},{2,3},{3,4},{4,5},{5,6},{6,7},{7,0},{8,9},{9,10},{10,1... | collective-permute-start | bytes 1622024 | tf_op jit(solution)/shard_map/ppermute | solution.py:62
  43.7 3.2 %collective-permute-done.21.refs_22_ = bf16[264,1024]{1,0:T(8,128)(2,1)S(1)} collective-permute-done((bf16[264,1024]{1,0:T(8,128)(2,1)S(1)}, bf16[264,1024]{1,0:T(8,128)(2,1)S(1)}, u32[]{:S(2)}, u32[]{:S(2)}) %collective-permute-start.21) | collective-permute-done | bytes 540704 | tf_op jit(solution)/shard_map/ppermute | solution.py:54
  46.9 5.3 %collective-permute-done.25.refs_26_ = bf16[264,1024]{1,0:T(8,128)(2,1)S(1)} collective-permute-done((bf16[264,1024]{1,0:T(8,128)(2,1)S(1)}, bf16[264,1024]{1,0:T(8,128)(2,1)S(1)}, u32[]{:S(2)}, u32[]{:S(2)}) %collective-permute-start.25) | collective-permute-done | bytes 540704 | tf_op jit(solution)/shard_map/ppermute | solution.py:54
  52.2 3.7 %collective-permute-done.29.refs_30_ = bf16[264,1024]{1,0:T(8,128)(2,1)S(1)} collective-permute-done((bf16[264,1024]{1,0:T(8,128)(2,1)S(1)}, bf16[264,1024]{1,0:T(8,128)(2,1)S(1)}, u32[]{:S(2)}, u32[]{:S(2)}) %collective-permute-start.29) | collective-permute-done | bytes 540704 | tf_op jit(solution)/shard_map/ppermute | solution.py:54
  55.9 0.5 collective-permute-start.16
  56.4 2.8 %collective-permute-start.27 = (bf16[264,1024]{1,0:T(8,128)(2,1)S(1)}, bf16[264,1024]{1,0:T(8,128)(2,1)}, u32[]{:S(2)}, u32[]{:S(2)}) collective-permute-start(bf16[264,1024]{1,0:T(8,128)(2,1)S(1)} %collective-permute-done.19.refs_20_), channel_id=1, source_target_pairs={{0,48},{8,56},{16,0},{24,8},{32,16},{40,24},{48,32},{56,40},{64,11... | collective-permute-start | bytes 1622024 | tf_op jit(solution)/shard_map/ppermute | solution.py:54
  59.2 1.7 %collective-permute-start.31 = (bf16[264,1024]{1,0:T(8,128)(2,1)S(1)}, bf16[264,1024]{1,0:T(8,128)(2,1)}, u32[]{:S(2)}, u32[]{:S(2)}) collective-permute-start(bf16[264,1024]{1,0:T(8,128)(2,1)S(1)} %collective-permute-done.23.refs_24_), channel_id=1, source_target_pairs={{0,192},{8,200},{16,208},{24,216},{32,224},{40,232},{48,240},{56,2... | collective-permute-start | bytes 1622024 | tf_op jit(solution)/shard_map/ppermute | solution.py:54
  61.0 0.4 collective-permute-start.35
  61.4 9.6 %collective-permute-done.27.refs_28_ = bf16[264,1024]{1,0:T(8,128)(2,1)} collective-permute-done((bf16[264,1024]{1,0:T(8,128)(2,1)S(1)}, bf16[264,1024]{1,0:T(8,128)(2,1)}, u32[]{:S(2)}, u32[]{:S(2)}) %collective-permute-start.27) | collective-permute-done | bytes 540704 | tf_op jit(solution)/shard_map/ppermute | solution.py:54
  71.0 2.3 %collective-permute-done.31.refs_32_ = bf16[264,1024]{1,0:T(8,128)(2,1)} collective-permute-done((bf16[264,1024]{1,0:T(8,128)(2,1)S(1)}, bf16[264,1024]{1,0:T(8,128)(2,1)}, u32[]{:S(2)}, u32[]{:S(2)}) %collective-permute-start.31) | collective-permute-done | bytes 540704 | tf_op jit(solution)/shard_map/ppermute | solution.py:54
  73.3 2.7 %collective-permute-done.33.refs_34_ = bf16[264,1024]{1,0:T(8,128)(2,1)} collective-permute-done((bf16[264,1024]{1,0:T(8,128)(2,1)S(1)}, bf16[264,1024]{1,0:T(8,128)(2,1)}, u32[]{:S(2)}, u32[]{:S(2)}) %collective-permute-start.33) | collective-permute-done | bytes 540704 | tf_op jit(solution)/shard_map/ppermute | solution.py:54
  76.0 4.5 %collective-permute-start.5 = (bf16[264,1024]{1,0:T(8,128)(2,1)S(1)}, bf16[264,1024]{1,0:T(8,128)(2,1)S(1)}, u32[]{:S(2)}, u32[]{:S(2)}) collective-permute-start(bf16[264,1024]{1,0:T(8,128)(2,1)S(1)} %collective-permute-done.3.refs_4_), channel_id=1, source_target_pairs={{0,7},{1,0},{2,1},{3,2},{4,3},{5,4},{6,5},{7,6},{8,15},{9,8},{10,9... | collective-permute-start | bytes 1622024 | tf_op jit(solution)/shard_map/ppermute | solution.py:62
  80.6 0.5 collective-permute-start.26
  81.1 0.1 collective-permute-start.30
  81.2 9.6 %collective-permute-done.5.refs_6_ = bf16[264,1024]{1,0:T(8,128)(2,1)S(1)} collective-permute-done((bf16[264,1024]{1,0:T(8,128)(2,1)S(1)}, bf16[264,1024]{1,0:T(8,128)(2,1)S(1)}, u32[]{:S(2)}, u32[]{:S(2)}) %collective-permute-start.5) | collective-permute-done | bytes 540704 | tf_op jit(solution)/shard_map/ppermute | solution.py:62
  91.0 2.2 %collective-permute-start.37 = (bf16[264,1024]{1,0:T(8,128)(2,1)}, bf16[264,1024]{1,0:T(8,128)(2,1)}, u32[]{:S(2)}, u32[]{:S(2)}) collective-permute-start(bf16[264,1024]{1,0:T(8,128)(2,1)} %collective-permute-done.27.refs_28_), channel_id=1, source_target_pairs={{0,192},{8,200},{16,208},{24,216},{32,224},{40,232},{48,240},{56,2... | collective-permute-start | bytes 1622024 | tf_op jit(solution)/shard_map/ppermute | solution.py:54
  93.2 2.6 %collective-permute-start.7 = (bf16[136,1024]{1,0:T(8,128)(2,1)S(1)}, bf16[136,1024]{1,0:T(8,128)(2,1)S(1)}, u32[]{:S(2)}, u32[]{:S(2)}) collective-permute-start(bf16[136,1024]{1,0:T(8,128)(2,1)S(1)} %slice.9), channel_id=1, source_target_pairs={{0,7},{1,0},{2,1},{3,2},{4,3},{5,4},{6,5},{7,6},{8,15},{9,8},{10,9... | collective-permute-start | bytes 835592 | tf_op jit(solution)/shard_map/ppermute | solution.py:62
  96.0 0.3 collective-permute-start.28
  96.3 0.5 collective-permute-start.32
  96.8 7.3 %collective-permute-done.6.refs_7_ = bf16[128,1024]{1,0:T(8,128)(2,1)S(1)} collective-permute-done((bf16[128,1024]{1,0:T(8,128)(2,1)S(1)}, bf16[128,1024]{1,0:T(8,128)(2,1)S(1)}, u32[]{:S(2)}, u32[]{:S(2)}) %collective-permute-start.6) | collective-permute-done | bytes 262176 | tf_op jit(solution)/shard_map/ppermute | solution.py:62
  104.1 0.6 collective-permute-start.36
  104.8 0.6 pad_add_fusion.where_ref
  105.4 0.9 collective-permute-done.34.refs_35_
  106.3 0.8 collective-permute-done.36.refs_37_
  107.1 0.8 collective-permute-done.38.refs_39_
  107.9 20.1 %compare.36 = f32[8,1,256]{2,1,0:T(1,128)} custom-call(s32[2]{0:T(128)} %pad_add_fusion.where_ref, s32[32,32]{1,0:T(8,128)} %pattern_ref.1, bf16[264,1024]{1,0:T(8,128)(2,1)} %copy-done.1, bf16[264,1024]{1,0:T(8,128)(2,1)} %copy-done.10, bf16[264,1024]{1,0:T(8,128)(2,1)} %copy-done.9, bf16[264,1024]{1,0:T(8,128)(2,1)} %copy-done.19, ...), custom_call_target="tpu_custom_call" | custom-call | flops 8589934592 | bytes 20971520 | tf_op jit(solution)/shard_map/compare/pallas_call | solution.py:260
  128.0 13.6 %all_to_all.5 = f32[8,1,256]{2,1,0:T(1,128)S(1)} all-to-all(f32[8,1,256]{2,1,0:T(1,128)} %compare.36), channel_id=1, replica_groups=mesh['grp'=32,'own'=8] {'own'}, dimensions={0} | all-to-all | bytes 16384 | tf_op jit(solution)/shard_map/all_to_all | solution.py:329
  141.7 0.7 reshape.28
  (113 shorter events, 0.9 us)
Async XLA Ops:
  2.3 102.5 %copy-start.1 = (bf16[264,1024]{1,0:T(8,128)(2,1)}, bf16[264,1024]{1,0:T(8,128)(2,1)S(1)}, u32[]{:S(2)}) copy-start(bf16[264,1024]{1,0:T(8,128)(2,1)S(1)} %pad_maximum_fusion.refs_0_) | copy-start | bytes 1622020
  2.3 14.6 %collective-permute-start.15 = (bf16[264,1024]{1,0:T(8,128)(2,1)S(1)}, bf16[264,1024]{1,0:T(8,128)(2,1)S(1)}, u32[]{:S(2)}, u32[]{:S(2)}) collective-permute-start(bf16[264,1024]{1,0:T(8,128)(2,1)S(1)} %pad_maximum_fusion.refs_0_), channel_id=1, source_target_pairs={{0,192},{8,200},{16,208},{24,216},{32,224},{40,232},{48,240},{56,2... | collective-permute-start | bytes 1622024 | tf_op jit(solution)/shard_map/ppermute | solution.py:54
  5.4 14.9 %collective-permute-start.9 = (bf16[264,1024]{1,0:T(8,128)(2,1)S(1)}, bf16[264,1024]{1,0:T(8,128)(2,1)S(1)}, u32[]{:S(2)}, u32[]{:S(2)}) collective-permute-start(bf16[264,1024]{1,0:T(8,128)(2,1)S(1)} %pad_maximum_fusion.refs_0_), channel_id=1, source_target_pairs={{0,16},{8,24},{16,32},{24,40},{32,48},{40,56},{48,0},{56,8},{64,80... | collective-permute-start | bytes 1622024 | tf_op jit(solution)/shard_map/ppermute | solution.py:54
  6.9 14.7 %collective-permute-start.13 = (bf16[264,1024]{1,0:T(8,128)(2,1)S(1)}, bf16[264,1024]{1,0:T(8,128)(2,1)S(1)}, u32[]{:S(2)}, u32[]{:S(2)}) collective-permute-start(bf16[264,1024]{1,0:T(8,128)(2,1)S(1)} %pad_maximum_fusion.refs_0_), channel_id=1, source_target_pairs={{0,64},{8,72},{16,80},{24,88},{32,96},{40,104},{48,112},{56,120},{... | collective-permute-start | bytes 1622024 | tf_op jit(solution)/shard_map/ppermute | solution.py:54
  6.9 16.4 %collective-permute-start.11 = (bf16[264,1024]{1,0:T(8,128)(2,1)S(1)}, bf16[264,1024]{1,0:T(8,128)(2,1)S(1)}, u32[]{:S(2)}, u32[]{:S(2)}) collective-permute-start(bf16[264,1024]{1,0:T(8,128)(2,1)S(1)} %pad_maximum_fusion.refs_0_), channel_id=1, source_target_pairs={{0,48},{8,56},{16,0},{24,8},{32,16},{40,24},{48,32},{56,40},{64,11... | collective-permute-start | bytes 1622024 | tf_op jit(solution)/shard_map/ppermute | solution.py:54
  8.6 16.8 %collective-permute-start.1 = (bf16[264,1024]{1,0:T(8,128)(2,1)S(1)}, bf16[264,1024]{1,0:T(8,128)(2,1)S(1)}, u32[]{:S(2)}, u32[]{:S(2)}) collective-permute-start(bf16[264,1024]{1,0:T(8,128)(2,1)S(1)} %pad_maximum_fusion.refs_0_), channel_id=1, source_target_pairs={{0,7},{1,0},{2,1},{3,2},{4,3},{5,4},{6,5},{7,6},{8,15},{9,8},{10,9... | collective-permute-start | bytes 1622024 | tf_op jit(solution)/shard_map/ppermute | solution.py:62
  16.9 91.0 %copy-start.5 = (bf16[264,1024]{1,0:T(8,128)(2,1)}, bf16[264,1024]{1,0:T(8,128)(2,1)S(1)}, u32[]{:S(2)}) copy-start(bf16[264,1024]{1,0:T(8,128)(2,1)S(1)} %collective-permute-done.15.refs_16_) | copy-start | bytes 1622020
  16.9 13.2 %collective-permute-start = (bf16[264,1024]{1,0:T(8,128)(2,1)S(1)}, bf16[264,1024]{1,0:T(8,128)(2,1)S(1)}, u32[]{:S(2)}, u32[]{:S(2)}) collective-permute-start(bf16[264,1024]{1,0:T(8,128)(2,1)S(1)} %pad_maximum_fusion.refs_0_), channel_id=1, source_target_pairs={{0,1},{1,2},{2,3},{3,4},{4,5},{5,6},{6,7},{7,0},{8,9},{9,10},{10,1... | collective-permute-start | bytes 1622024 | tf_op jit(solution)/shard_map/ppermute | solution.py:62
  20.3 87.6 %copy-start.6 = (bf16[264,1024]{1,0:T(8,128)(2,1)}, bf16[264,1024]{1,0:T(8,128)(2,1)S(1)}, u32[]{:S(2)}) copy-start(bf16[264,1024]{1,0:T(8,128)(2,1)S(1)} %collective-permute-done.9.refs_10_) | copy-start | bytes 1622020
  20.3 10.8 %collective-permute-start.8 = (bf16[264,1024]{1,0:T(8,128)(2,1)S(1)}, bf16[264,1024]{1,0:T(8,128)(2,1)S(1)}, u32[]{:S(2)}, u32[]{:S(2)}) collective-permute-start(bf16[264,1024]{1,0:T(8,128)(2,1)S(1)} %pad_maximum_fusion.refs_0_), channel_id=1, source_target_pairs={{0,8},{8,0},{16,24},{24,16},{32,40},{40,32},{48,56},{56,48},{64,72... | collective-permute-start | bytes 1622024 | tf_op jit(solution)/shard_map/ppermute | solution.py:58
  21.5 86.4 %copy-start.7 = (bf16[264,1024]{1,0:T(8,128)(2,1)}, bf16[264,1024]{1,0:T(8,128)(2,1)S(1)}, u32[]{:S(2)}) copy-start(bf16[264,1024]{1,0:T(8,128)(2,1)S(1)} %collective-permute-done.13.refs_14_) | copy-start | bytes 1622020
  21.5 13.5 %collective-permute-start.19 = (bf16[264,1024]{1,0:T(8,128)(2,1)S(1)}, bf16[264,1024]{1,0:T(8,128)(2,1)S(1)}, u32[]{:S(2)}, u32[]{:S(2)}) collective-permute-start(bf16[264,1024]{1,0:T(8,128)(2,1)S(1)} %collective-permute-done.15.refs_16_), channel_id=1, source_target_pairs={{0,48},{8,56},{16,0},{24,8},{32,16},{40,24},{48,32},{56,40},{64,11... | collective-permute-start | bytes 1622024 | tf_op jit(solution)/shard_map/ppermute | solution.py:54
  23.3 67.6 %copy-start.8 = (bf16[264,1024]{1,0:T(8,128)(2,1)}, bf16[264,1024]{1,0:T(8,128)(2,1)S(1)}, u32[]{:S(2)}) copy-start(bf16[264,1024]{1,0:T(8,128)(2,1)S(1)} %collective-permute-done.11.refs_12_) | copy-start | bytes 1622020
  23.3 13.9 %collective-permute-start.23 = (bf16[264,1024]{1,0:T(8,128)(2,1)S(1)}, bf16[264,1024]{1,0:T(8,128)(2,1)S(1)}, u32[]{:S(2)}, u32[]{:S(2)}) collective-permute-start(bf16[264,1024]{1,0:T(8,128)(2,1)S(1)} %collective-permute-done.9.refs_10_), channel_id=1, source_target_pairs={{0,192},{8,200},{16,208},{24,216},{32,224},{40,232},{48,240},{56,2... | collective-permute-start | bytes 1622024 | tf_op jit(solution)/shard_map/ppermute | solution.py:54
  25.4 65.5 %copy-start.9 = (bf16[264,1024]{1,0:T(8,128)(2,1)}, bf16[264,1024]{1,0:T(8,128)(2,1)S(1)}, u32[]{:S(2)}) copy-start(bf16[264,1024]{1,0:T(8,128)(2,1)S(1)} %collective-permute-done.1.refs_2_) | copy-start | bytes 1622020
  25.4 16.4 %collective-permute-start.17 = (bf16[264,1024]{1,0:T(8,128)(2,1)S(1)}, bf16[264,1024]{1,0:T(8,128)(2,1)S(1)}, u32[]{:S(2)}, u32[]{:S(2)}) collective-permute-start(bf16[264,1024]{1,0:T(8,128)(2,1)S(1)} %collective-permute-done.13.refs_14_), channel_id=1, source_target_pairs={{0,16},{8,24},{16,32},{24,40},{32,48},{40,56},{48,0},{56,8},{64,80... | collective-permute-start | bytes 1622024 | tf_op jit(solution)/shard_map/ppermute | solution.py:54
  30.1 60.8 %copy-start.10 = (bf16[264,1024]{1,0:T(8,128)(2,1)}, bf16[264,1024]{1,0:T(8,128)(2,1)S(1)}, u32[]{:S(2)}) copy-start(bf16[264,1024]{1,0:T(8,128)(2,1)S(1)} %collective-permute-done.refs_1_) | copy-start | bytes 1622020
  30.1 16.8 %collective-permute-start.21 = (bf16[264,1024]{1,0:T(8,128)(2,1)S(1)}, bf16[264,1024]{1,0:T(8,128)(2,1)S(1)}, u32[]{:S(2)}, u32[]{:S(2)}) collective-permute-start(bf16[264,1024]{1,0:T(8,128)(2,1)S(1)} %collective-permute-done.11.refs_12_), channel_id=1, source_target_pairs={{0,64},{8,72},{16,80},{24,88},{32,96},{40,104},{48,112},{56,120},{... | collective-permute-start | bytes 1622024 | tf_op jit(solution)/shard_map/ppermute | solution.py:54
  31.1 59.8 %copy-start.11 = (bf16[264,1024]{1,0:T(8,128)(2,1)}, bf16[264,1024]{1,0:T(8,128)(2,1)S(1)}, u32[]{:S(2)}) copy-start(bf16[264,1024]{1,0:T(8,128)(2,1)S(1)} %collective-permute-done.8.refs_9_) | copy-start | bytes 1622020
  31.1 21.1 %collective-permute-start.25 = (bf16[264,1024]{1,0:T(8,128)(2,1)S(1)}, bf16[264,1024]{1,0:T(8,128)(2,1)S(1)}, u32[]{:S(2)}, u32[]{:S(2)}) collective-permute-start(bf16[264,1024]{1,0:T(8,128)(2,1)S(1)} %collective-permute-done.9.refs_10_), channel_id=1, source_target_pairs={{0,16},{8,24},{16,32},{24,40},{32,48},{40,56},{48,0},{56,8},{64,80... | collective-permute-start | bytes 1622024 | tf_op jit(solution)/shard_map/ppermute | solution.py:54
  35.0 20.9 %collective-permute-start.29 = (bf16[264,1024]{1,0:T(8,128)(2,1)S(1)}, bf16[264,1024]{1,0:T(8,128)(2,1)S(1)}, u32[]{:S(2)}, u32[]{:S(2)}) collective-permute-start(bf16[264,1024]{1,0:T(8,128)(2,1)S(1)} %collective-permute-done.13.refs_14_), channel_id=1, source_target_pairs={{0,64},{8,72},{16,80},{24,88},{32,96},{40,104},{48,112},{56,120},{... | collective-permute-start | bytes 1622024 | tf_op jit(solution)/shard_map/ppermute | solution.py:54
  37.2 18.7 %collective-permute-start.3 = (bf16[264,1024]{1,0:T(8,128)(2,1)S(1)}, bf16[264,1024]{1,0:T(8,128)(2,1)S(1)}, u32[]{:S(2)}, u32[]{:S(2)}) collective-permute-start(bf16[264,1024]{1,0:T(8,128)(2,1)S(1)} %collective-permute-done.1.refs_2_), channel_id=1, source_target_pairs={{0,7},{1,0},{2,1},{3,2},{4,3},{5,4},{6,5},{7,6},{8,15},{9,8},{10,9... | collective-permute-start | bytes 1622024 | tf_op jit(solution)/shard_map/ppermute | solution.py:62
  41.8 14.7 %collective-permute-start.2 = (bf16[264,1024]{1,0:T(8,128)(2,1)S(1)}, bf16[264,1024]{1,0:T(8,128)(2,1)S(1)}, u32[]{:S(2)}, u32[]{:S(2)}) collective-permute-start(bf16[264,1024]{1,0:T(8,128)(2,1)S(1)} %collective-permute-done.refs_1_), channel_id=1, source_target_pairs={{0,1},{1,2},{2,3},{3,4},{4,5},{5,6},{6,7},{7,0},{8,9},{9,10},{10,1... | collective-permute-start | bytes 1622024 | tf_op jit(solution)/shard_map/ppermute | solution.py:62
  46.9 57.2 %copy-start.15 = (bf16[264,1024]{1,0:T(8,128)(2,1)}, bf16[264,1024]{1,0:T(8,128)(2,1)S(1)}, u32[]{:S(2)}) copy-start(bf16[264,1024]{1,0:T(8,128)(2,1)S(1)} %collective-permute-done.21.refs_22_) | copy-start | bytes 1622020
  46.9 12.3 %collective-permute-start.10 = (bf16[264,1024]{1,0:T(8,128)(2,1)S(1)}, bf16[264,1024]{1,0:T(8,128)(2,1)S(1)}, u32[]{:S(2)}, u32[]{:S(2)}) collective-permute-start(bf16[264,1024]{1,0:T(8,128)(2,1)S(1)} %collective-permute-done.9.refs_10_), channel_id=1, source_target_pairs={{0,8},{8,0},{16,24},{24,16},{32,40},{40,32},{48,56},{56,48},{64,72... | collective-permute-start | bytes 1622024 | tf_op jit(solution)/shard_map/ppermute | solution.py:58
  52.2 8.7 %collective-permute-start.14 = (bf16[264,1024]{1,0:T(8,128)(2,1)S(1)}, bf16[264,1024]{1,0:T(8,128)(2,1)S(1)}, u32[]{:S(2)}, u32[]{:S(2)}) collective-permute-start(bf16[264,1024]{1,0:T(8,128)(2,1)S(1)} %collective-permute-done.13.refs_14_), channel_id=1, source_target_pairs={{0,8},{8,0},{16,24},{24,16},{32,40},{40,32},{48,56},{56,48},{64,72... | collective-permute-start | bytes 1622024 | tf_op jit(solution)/shard_map/ppermute | solution.py:58
  55.9 5.0 %collective-permute-start.12 = (bf16[264,1024]{1,0:T(8,128)(2,1)S(1)}, bf16[264,1024]{1,0:T(8,128)(2,1)S(1)}, u32[]{:S(2)}, u32[]{:S(2)}) collective-permute-start(bf16[264,1024]{1,0:T(8,128)(2,1)S(1)} %collective-permute-done.11.refs_12_), channel_id=1, source_target_pairs={{0,8},{8,0},{16,24},{24,16},{32,40},{40,32},{48,56},{56,48},{64,72... | collective-permute-start | bytes 1622024 | tf_op jit(solution)/shard_map/ppermute | solution.py:58
  55.9 5.4 %collective-permute-start.16 = (bf16[264,1024]{1,0:T(8,128)(2,1)S(1)}, bf16[264,1024]{1,0:T(8,128)(2,1)S(1)}, u32[]{:S(2)}, u32[]{:S(2)}) collective-permute-start(bf16[264,1024]{1,0:T(8,128)(2,1)S(1)} %collective-permute-done.15.refs_16_), channel_id=1, source_target_pairs={{0,8},{8,0},{16,24},{24,16},{32,40},{40,32},{48,56},{56,48},{64,72... | collective-permute-start | bytes 1622024 | tf_op jit(solution)/shard_map/ppermute | solution.py:58
  56.4 14.6 %collective-permute-start.27 = (bf16[264,1024]{1,0:T(8,128)(2,1)S(1)}, bf16[264,1024]{1,0:T(8,128)(2,1)}, u32[]{:S(2)}, u32[]{:S(2)}) collective-permute-start(bf16[264,1024]{1,0:T(8,128)(2,1)S(1)} %collective-permute-done.19.refs_20_), channel_id=1, source_target_pairs={{0,48},{8,56},{16,0},{24,8},{32,16},{40,24},{48,32},{56,40},{64,11... | collective-permute-start | bytes 1622024 | tf_op jit(solution)/shard_map/ppermute | solution.py:54
  59.2 14.1 %collective-permute-start.31 = (bf16[264,1024]{1,0:T(8,128)(2,1)S(1)}, bf16[264,1024]{1,0:T(8,128)(2,1)}, u32[]{:S(2)}, u32[]{:S(2)}) collective-permute-start(bf16[264,1024]{1,0:T(8,128)(2,1)S(1)} %collective-permute-done.23.refs_24_), channel_id=1, source_target_pairs={{0,192},{8,200},{16,208},{24,216},{32,224},{40,232},{48,240},{56,2... | collective-permute-start | bytes 1622024 | tf_op jit(solution)/shard_map/ppermute | solution.py:54
  61.0 15.0 %collective-permute-start.33 = (bf16[264,1024]{1,0:T(8,128)(2,1)S(1)}, bf16[264,1024]{1,0:T(8,128)(2,1)}, u32[]{:S(2)}, u32[]{:S(2)}) collective-permute-start(bf16[264,1024]{1,0:T(8,128)(2,1)S(1)} %collective-permute-done.17.refs_18_), channel_id=1, source_target_pairs={{0,16},{8,24},{16,32},{24,40},{32,48},{40,56},{48,0},{56,8},{64,80... | collective-permute-start | bytes 1622024 | tf_op jit(solution)/shard_map/ppermute | solution.py:54
  61.0 19.5 %collective-permute-start.35 = (bf16[264,1024]{1,0:T(8,128)(2,1)S(1)}, bf16[264,1024]{1,0:T(8,128)(2,1)}, u32[]{:S(2)}, u32[]{:S(2)}) collective-permute-start(bf16[264,1024]{1,0:T(8,128)(2,1)S(1)} %collective-permute-done.21.refs_22_), channel_id=1, source_target_pairs={{0,64},{8,72},{16,80},{24,88},{32,96},{40,104},{48,112},{56,120},{... | collective-permute-start | bytes 1622024 | tf_op jit(solution)/shard_map/ppermute | solution.py:54
  61.3 19.2 %collective-permute-start.18 = (bf16[264,1024]{1,0:T(8,128)(2,1)S(1)}, bf16[264,1024]{1,0:T(8,128)(2,1)S(1)}, u32[]{:S(2)}, u32[]{:S(2)}) collective-permute-start(bf16[264,1024]{1,0:T(8,128)(2,1)S(1)} %collective-permute-done.17.refs_18_), channel_id=1, source_target_pairs={{0,8},{8,0},{16,24},{24,16},{32,40},{40,32},{48,56},{56,48},{64,72... | collective-permute-start | bytes 1622024 | tf_op jit(solution)/shard_map/ppermute | solution.py:58
  71.0 9.6 %collective-permute-start.24 = (bf16[264,1024]{1,0:T(8,128)(2,1)S(1)}, bf16[264,1024]{1,0:T(8,128)(2,1)S(1)}, u32[]{:S(2)}, u32[]{:S(2)}) collective-permute-start(bf16[264,1024]{1,0:T(8,128)(2,1)S(1)} %collective-permute-done.23.refs_24_), channel_id=1, source_target_pairs={{0,8},{8,0},{16,24},{24,16},{32,40},{40,32},{48,56},{56,48},{64,72... | collective-permute-start | bytes 1622024 | tf_op jit(solution)/shard_map/ppermute | solution.py:58
  73.3 7.8 %collective-permute-start.20 = (bf16[264,1024]{1,0:T(8,128)(2,1)S(1)}, bf16[264,1024]{1,0:T(8,128)(2,1)S(1)}, u32[]{:S(2)}, u32[]{:S(2)}) collective-permute-start(bf16[264,1024]{1,0:T(8,128)(2,1)S(1)} %collective-permute-done.19.refs_20_), channel_id=1, source_target_pairs={{0,8},{8,0},{16,24},{24,16},{32,40},{40,32},{48,56},{56,48},{64,72... | collective-permute-start | bytes 1622024 | tf_op jit(solution)/shard_map/ppermute | solution.py:58
  76.0 14.9 %collective-permute-start.5 = (bf16[264,1024]{1,0:T(8,128)(2,1)S(1)}, bf16[264,1024]{1,0:T(8,128)(2,1)S(1)}, u32[]{:S(2)}, u32[]{:S(2)}) collective-permute-start(bf16[264,1024]{1,0:T(8,128)(2,1)S(1)} %collective-permute-done.3.refs_4_), channel_id=1, source_target_pairs={{0,7},{1,0},{2,1},{3,2},{4,3},{5,4},{6,5},{7,6},{8,15},{9,8},{10,9... | collective-permute-start | bytes 1622024 | tf_op jit(solution)/shard_map/ppermute | solution.py:62
  80.5 12.7 %collective-permute-start.4 = (bf16[264,1024]{1,0:T(8,128)(2,1)S(1)}, bf16[264,1024]{1,0:T(8,128)(2,1)S(1)}, u32[]{:S(2)}, u32[]{:S(2)}) collective-permute-start(bf16[264,1024]{1,0:T(8,128)(2,1)S(1)} %collective-permute-done.2.refs_3_), channel_id=1, source_target_pairs={{0,1},{1,2},{2,3},{3,4},{4,5},{5,6},{6,7},{7,0},{8,9},{9,10},{10,1... | collective-permute-start | bytes 1622024 | tf_op jit(solution)/shard_map/ppermute | solution.py:62
  80.5 15.3 %collective-permute-start.22 = (bf16[264,1024]{1,0:T(8,128)(2,1)S(1)}, bf16[264,1024]{1,0:T(8,128)(2,1)S(1)}, u32[]{:S(2)}, u32[]{:S(2)}) collective-permute-start(bf16[264,1024]{1,0:T(8,128)(2,1)S(1)} %collective-permute-done.21.refs_22_), channel_id=1, source_target_pairs={{0,8},{8,0},{16,24},{24,16},{32,40},{40,32},{48,56},{56,48},{64,72... | collective-permute-start | bytes 1622024 | tf_op jit(solution)/shard_map/ppermute | solution.py:58
  80.6 15.3 %collective-permute-start.26 = (bf16[264,1024]{1,0:T(8,128)(2,1)S(1)}, bf16[264,1024]{1,0:T(8,128)(2,1)S(1)}, u32[]{:S(2)}, u32[]{:S(2)}) collective-permute-start(bf16[264,1024]{1,0:T(8,128)(2,1)S(1)} %collective-permute-done.25.refs_26_), channel_id=1, source_target_pairs={{0,8},{8,0},{16,24},{24,16},{32,40},{40,32},{48,56},{56,48},{64,72... | collective-permute-start | bytes 1622024 | tf_op jit(solution)/shard_map/ppermute | solution.py:58
  81.1 15.2 %collective-permute-start.30 = (bf16[264,1024]{1,0:T(8,128)(2,1)S(1)}, bf16[264,1024]{1,0:T(8,128)(2,1)S(1)}, u32[]{:S(2)}, u32[]{:S(2)}) collective-permute-start(bf16[264,1024]{1,0:T(8,128)(2,1)S(1)} %collective-permute-done.29.refs_30_), channel_id=1, source_target_pairs={{0,8},{8,0},{16,24},{24,16},{32,40},{40,32},{48,56},{56,48},{64,72... | collective-permute-start | bytes 1622024 | tf_op jit(solution)/shard_map/ppermute | solution.py:58
  91.0 13.8 %collective-permute-start.37 = (bf16[264,1024]{1,0:T(8,128)(2,1)}, bf16[264,1024]{1,0:T(8,128)(2,1)}, u32[]{:S(2)}, u32[]{:S(2)}) collective-permute-start(bf16[264,1024]{1,0:T(8,128)(2,1)} %collective-permute-done.27.refs_28_), channel_id=1, source_target_pairs={{0,192},{8,200},{16,208},{24,216},{32,224},{40,232},{48,240},{56,2... | collective-permute-start | bytes 1622024 | tf_op jit(solution)/shard_map/ppermute | solution.py:54
  93.2 10.8 %collective-permute-start.7 = (bf16[136,1024]{1,0:T(8,128)(2,1)S(1)}, bf16[136,1024]{1,0:T(8,128)(2,1)S(1)}, u32[]{:S(2)}, u32[]{:S(2)}) collective-permute-start(bf16[136,1024]{1,0:T(8,128)(2,1)S(1)} %slice.9), channel_id=1, source_target_pairs={{0,7},{1,0},{2,1},{3,2},{4,3},{5,4},{6,5},{7,6},{8,15},{9,8},{10,9... | collective-permute-start | bytes 835592 | tf_op jit(solution)/shard_map/ppermute | solution.py:62
  95.8 8.2 %collective-permute-start.6 = (bf16[128,1024]{1,0:T(8,128)(2,1)S(1)}, bf16[128,1024]{1,0:T(8,128)(2,1)S(1)}, u32[]{:S(2)}, u32[]{:S(2)}) collective-permute-start(bf16[128,1024]{1,0:T(8,128)(2,1)S(1)} %slice.8), channel_id=1, source_target_pairs={{0,1},{1,2},{2,3},{3,4},{4,5},{5,6},{6,7},{7,0},{8,9},{9,10},{10,1... | collective-permute-start | bytes 786440 | tf_op jit(solution)/shard_map/ppermute | solution.py:62
  96.0 9.5 %collective-permute-start.28 = (bf16[264,1024]{1,0:T(8,128)(2,1)}, bf16[264,1024]{1,0:T(8,128)(2,1)}, u32[]{:S(2)}, u32[]{:S(2)}) collective-permute-start(bf16[264,1024]{1,0:T(8,128)(2,1)} %collective-permute-done.27.refs_28_), channel_id=1, source_target_pairs={{0,8},{8,0},{16,24},{24,16},{32,40},{40,32},{48,56},{56,48},{64,72... | collective-permute-start | bytes 1622024 | tf_op jit(solution)/shard_map/ppermute | solution.py:58
  96.3 9.1 %collective-permute-start.32 = (bf16[264,1024]{1,0:T(8,128)(2,1)}, bf16[264,1024]{1,0:T(8,128)(2,1)}, u32[]{:S(2)}, u32[]{:S(2)}) collective-permute-start(bf16[264,1024]{1,0:T(8,128)(2,1)} %collective-permute-done.31.refs_32_), channel_id=1, source_target_pairs={{0,8},{8,0},{16,24},{24,16},{32,40},{40,32},{48,56},{56,48},{64,72... | collective-permute-start | bytes 1622024 | tf_op jit(solution)/shard_map/ppermute | solution.py:58
  104.1 2.3 %collective-permute-start.34 = (bf16[264,1024]{1,0:T(8,128)(2,1)}, bf16[264,1024]{1,0:T(8,128)(2,1)}, u32[]{:S(2)}, u32[]{:S(2)}) collective-permute-start(bf16[264,1024]{1,0:T(8,128)(2,1)} %collective-permute-done.33.refs_34_), channel_id=1, source_target_pairs={{0,8},{8,0},{16,24},{24,16},{32,40},{40,32},{48,56},{56,48},{64,72... | collective-permute-start | bytes 1622024 | tf_op jit(solution)/shard_map/ppermute | solution.py:58
  104.1 3.0 %collective-permute-start.36 = (bf16[264,1024]{1,0:T(8,128)(2,1)}, bf16[264,1024]{1,0:T(8,128)(2,1)}, u32[]{:S(2)}, u32[]{:S(2)}) collective-permute-start(bf16[264,1024]{1,0:T(8,128)(2,1)} %collective-permute-done.35.refs_36_), channel_id=1, source_target_pairs={{0,8},{8,0},{16,24},{24,16},{32,40},{40,32},{48,56},{56,48},{64,72... | collective-permute-start | bytes 1622024 | tf_op jit(solution)/shard_map/ppermute | solution.py:58
  104.8 3.1 %collective-permute-start.38 = (bf16[264,1024]{1,0:T(8,128)(2,1)}, bf16[264,1024]{1,0:T(8,128)(2,1)}, u32[]{:S(2)}, u32[]{:S(2)}) collective-permute-start(bf16[264,1024]{1,0:T(8,128)(2,1)} %collective-permute-done.37.refs_38_), channel_id=1, source_target_pairs={{0,8},{8,0},{16,24},{24,16},{32,40},{40,32},{48,56},{56,48},{64,72... | collective-permute-start | bytes 1622024 | tf_op jit(solution)/shard_map/ppermute | solution.py:58
  (24 other events, 557.5 us)
where the time goes:
time: 144 us; the launch traced here: 142 us
  waiting for transfers between devices  69.1 us (48%)
  starting transfers between devices  35.4 us (25%)
  Pallas kernels  20.1 us (14%)
  blocking collectives  13.6 us (9%)
  other arithmetic  2.12 us (1%)
  local copies, waits for them, and re-layouts  1.54 us (1%)
    ppermute x15, waiting for transfers between devices, in_plane(): return lax.ppermute(value, 'grp', plane_pairs(dx, dy, 0))  45.1 us
    ppermute x8, waiting for transfers between devices, along(): lax.ppermute(value, 'own', [(i, (i + step) % count) for i in range(count)])  21.6 us
    pallas_call x1, Pallas kernels, compare(): pl.pallas_call(functools.partial(compare_kernel, queries, keys), out_shap...  20.1 us
    ppermute x15, starting transfers between devices, in_plane(): return lax.ppermute(value, 'grp', plane_pairs(dx, dy, 0))  19.8 us
    all_to_all x1, blocking collectives, search(): lax.all_to_all(best, 'own', split_axis=0, concat_axis=0, tiled=True)  13.6 us
    ppermute x8, starting transfers between devices, along(): lax.ppermute(value, 'own', [(i, (i + step) % count) for i in range(count)])  13 us
  transfers between devices with their start and end apart: 39, of which 19 were waited for; matrix products, arithmetic and copies ran while one was open for 0% of the time, Pallas kernels for 0%

commit v1 on v0

--- a/solution.py
+++ b/solution.py
@@ -11,7 +11,7 @@
 TILE = 32
 GROUP = 8
 ROWS = TILE * GROUP
-CHUNKS = (4 * ROWS, 5 * ROWS)
+CHUNKS = (26 * TILE, 34 * TILE)
 
 TREE = (
     ((0, 0), (1, 0)),
@@ -74,9 +74,9 @@
     arrays = refs[:n_ops]
     out_ref, q_raw, k_raw, q_col, k_col, acc, spread, meta, own_vec = refs[n_ops : n_ops + 9]
     own_s, k_base, q_next, k_next, q_order, q_own_s, k_order, sems = refs[n_ops + 9 : n_ops + 17]
-    q_rows, q_names, found_rows = refs[n_ops + 17 :]
+    q_rows, q_names, found_rows, allow_s = refs[n_ops + 17 :]
     n_q, n_k = len(queries), len(keys)
-    k_tiles, blocks = n_k * GROUP, n_q + OWNERS
+    blocks = n_q + OWNERS
     small, large = (chunk // TILE for chunk in CHUNKS)
     half = ROWS // 2
     group, depth = where_ref[0], where_ref[1]
@@ -101,10 +101,23 @@
             pltpu.make_async_copy(
                 arrays[ref].at[pl.ds(0, rows)], q_raw.at[pl.ds(to, rows)], sems.at[1]
             ).start()
+
+    def key_copy(i):
+        return pltpu.make_async_copy(
+            arrays[keys[i][0]].at[pl.ds(0, ROWS)], k_raw.at[pl.ds(i * ROWS, ROWS)], sems.at[2 + i]
+        )
+
+    allows = []
     for i in range(n_k):
-        pltpu.make_async_copy(
-            arrays[keys[i][0]].at[pl.ds(0, ROWS)], k_raw.at[pl.ds(i * ROWS, ROWS)], sems.at[2]
-        ).start()
+        _, dx, dy, flip = keys[i]
+        source = (((chip_y - dy) % SIDE) * SIDE + (chip_x - dx) % SIDE) * 2 + (core + flip) % 2
+        allows.append(pattern_ref[group, source])
+        allow_s[i] = allows[i]
+
+        @pl.when(allows[i] > 0)
+        def _(i=i):
+            key_copy(i).start()
+
     pltpu.make_async_copy(meta, meta, sems.at[0]).wait()
     for i in range(n_q + n_k):
         own_vec[i : i + 1, :] = meta[i].astype(jnp.float32)[1:2, :].astype(jnp.int32)
@@ -122,10 +135,7 @@
         q_col[i * ROWS : (i + 1) * ROWS, :] = column(label(i))
     q_col[n_q * ROWS :, :] = jnp.full((TILE, 128), -3.0, jnp.float32)
     for i in range(n_k):
-        _, dx, dy, flip = keys[i]
-        source = (((chip_y - dy) % SIDE) * SIDE + (chip_x - dx) % SIDE) * 2 + (core + flip) % 2
-        allowed = pattern_ref[group, source] > 0
-        k_col[i * ROWS : (i + 1) * ROWS, :] = column(jnp.where(allowed, label(n_q + i), -1.0))
+        k_col[i * ROWS : (i + 1) * ROWS, :] = column(label(n_q + i))
     found_rows[...] = jnp.full_like(found_rows, -1.0)
     to_scalar.wait()
 
@@ -143,7 +153,10 @@
         return carry
 
     def count_k(i, carry):
-        count(i, k_next)
+        @pl.when(allow_s[i - n_q] > 0)
+        def _():
+            count(i, k_next)
+
         return carry
 
     lax.fori_loop(0, n_q, count_q, 0)
@@ -172,11 +185,14 @@
         return carry
 
     def put_k(i, carry):
-        for j in range(GROUP):
-            o = own_s[n_q + i, j * TILE]
-            to = k_next[o]
-            k_next[o] = to + 1
-            k_order[to] = i * GROUP + j
+        @pl.when(allow_s[i] > 0)
+        def _():
+            for j in range(GROUP):
+                o = own_s[n_q + i, j * TILE]
+                to = k_next[o]
+                k_next[o] = to + 1
+                k_order[to] = i * GROUP + j
+
         return carry
 
     lax.fori_loop(0, n_q, put_q, 0)
@@ -197,7 +213,12 @@
         name = jnp.concatenate([names(t, -(1 << 20)) for t in tiles], axis=0)
         q_names[b] = jnp.transpose(name.astype(jnp.float32))[0:1, :].astype(jnp.int32)
     pltpu.make_async_copy(q_raw, q_raw, sems.at[1]).wait()
-    pltpu.make_async_copy(k_raw, k_raw, sems.at[2]).wait()
+    for i in range(n_k):
+
+        @pl.when(allows[i] > 0)
+        def _(i=i):
+            key_copy(i).wait()
+
 
     def block_step(b, carry):
         owner = q_own_s[b]
@@ -210,7 +231,7 @@
 
         def chunk_step(per, m):
             tiles = [
-                k_order[jnp.minimum(lo + m * per + i, k_tiles - 1)] for i in range(per)
+                k_order[jnp.minimum(lo + m * per + i, k_total - 1)] for i in range(per)
             ]
             block = jnp.concatenate([q_raw[tile_rows(t), :] for t in q_at], axis=0)
             scores = lax.dot_general(
@@ -232,7 +253,7 @@
 
         fits = here <= small
 
-        @pl.when(fits)
+        @pl.when(fits & (here > 0))
         def _():
             chunk_step(small, 0)
 
@@ -278,10 +299,11 @@
             pltpu.SMEM((blocks * GROUP,), jnp.int32),
             pltpu.SMEM((blocks,), jnp.int32),
             pltpu.SMEM((n_k * GROUP,), jnp.int32),
-            pltpu.SemaphoreType.DMA((3,)),
+            pltpu.SemaphoreType.DMA((2 + n_k,)),
             pltpu.VMEM((blocks, 1, ROWS), jnp.float32),
             pltpu.VMEM((blocks, 1, ROWS), jnp.int32),
             pltpu.VMEM((blocks, 1, ROWS), jnp.float32),
+            pltpu.SMEM((n_k,), jnp.int32),
         ],
         cost_estimate=pl.CostEstimate(
             flops=2 * n_q * n_k * ROWS * ROWS * width // 4,
@@ -305,16 +327,24 @@
     up, down = [shard], [shard]
     arrays = [shard]
     queries = [(0, 0, 0)]
-    for hop in range(1, n_own // 2):
+    last, half = n_own // 2, ROWS // 2
+    for hop in range(1, last - 1):
         up.append(along(up[-1], 1, n_own))
         down.append(along(down[-1], -1, n_own))
         at = len(arrays)
         queries += [(at, at, hop), (at + 1, at + 1, -hop)]
         arrays += [up[-1], down[-1]]
-    far_low = along(up[-1][: ROWS // 2], 1, n_own)
-    far_high = along(down[-1][ROWS // 2 :], -1, n_own)
-    queries.append((len(arrays), len(arrays) + 1, n_own // 2))
-    arrays += [far_low, far_high]
+    up_low = along(up[-1][:half], 1, n_own)
+    down_high = along(down[-1][half:], -1, n_own)
+    up_high = along(up[-1][half:], 1, n_own)
+    down_low = along(down[-1][:half], -1, n_own)
+    far_low = along(up_low, 1, n_own)
+    far_high = along(down_high, -1, n_own)
+    for low, high, step in (
+        (up_low, up_high, last - 1), (down_low, down_high, 1 - last), (far_low, far_high, last)
+    ):
+        queries.append((len(arrays), len(arrays) + 1, step))
+        arrays += [low, high]
 
     held = {(0, 0): shard}
     keys = [(0, 0, 0, 0), (len(arrays), 0, 0, 1)]

time: 144 us -> 140 us (0.972)
  waiting for transfers between devices: 69.1 us -> 57.5 us
  starting transfers between devices: 35.4 us -> 42.1 us
    ppermute x8 -> x10, starting transfers between devices: 13 us -> 21.8 us  [along(): lax.ppermute(value, 'own', [(i, (i + step) % count) for i in range(count)])]
    ppermute x15, waiting for transfers between devices: 45.1 us -> 37.1 us  [in_plane(): return lax.ppermute(value, 'grp', plane_pairs(dx, dy, 0))]
    ppermute x8 -> x10, waiting for transfers between devices: 21.6 us -> 18.9 us  [along(): lax.ppermute(value, 'own', [(i, (i + step) % count) for i in range(count)])]
    ppermute x15, starting transfers between devices: 19.8 us -> 17.8 us  [in_plane(): return lax.ppermute(value, 'grp', plane_pairs(dx, dy, 0))]
  transfers between devices with their start and end apart: 39 -> 41, of which waited for: 19 -> 18; matrix products, arithmetic and copies ran while one was open for 0% -> 1% of each run, Pallas kernels for 0% -> 0%
where the time goes in v1:
time: 140 us; the launch traced here: 139 us
  waiting for transfers between devices  57.5 us (41%)
  starting transfers between devices  42.1 us (30%)
  Pallas kernels  19.8 us (14%)
  blocking collectives  14.2 us (10%)
  local copies, waits for them, and re-layouts  2.36 us (2%)
  other arithmetic  2.18 us (2%)
    ppermute x15, waiting for transfers between devices, in_plane(): return lax.ppermute(value, 'grp', plane_pairs(dx, dy, 0))  37.1 us
    ppermute x10, starting transfers between devices, along(): lax.ppermute(value, 'own', [(i, (i + step) % count) for i in range(count)])  21.8 us
    pallas_call x1, Pallas kernels, compare(): pl.pallas_call(functools.partial(compare_kernel, queries, keys), out_shap...  19.8 us
    ppermute x10, waiting for transfers between devices, along(): lax.ppermute(value, 'own', [(i, (i + step) % count) for i in range(count)])  18.9 us
    ppermute x15, starting transfers between devices, in_plane(): return lax.ppermute(value, 'grp', plane_pairs(dx, dy, 0))  17.8 us
    all_to_all x1, blocking collectives, search(): lax.all_to_all(best, 'own', split_axis=0, concat_axis=0, tiled=True)  14.2 us
  transfers between devices with their start and end apart: 41, of which 18 were waited for; matrix products, arithmetic and copies ran while one was open for 1% of the time, Pallas kernels for 0%

profile of v1, /device:TPU:32, one launch (start us, length us, event | category | flops | bytes accessed | tf_op | source)
XLA Modules:
  0.0 138.5 jit_solution(5751836725393662936)
XLA Ops:
  0.0 1.3 fusion
  1.5 0.5 copy-done.34
  2.3 3.1 %collective-permute-start.17 = (bf16[264,1024]{1,0:T(8,128)(2,1)S(1)}, bf16[264,1024]{1,0:T(8,128)(2,1)S(1)}, u32[]{:S(2)}, u32[]{:S(2)}) collective-permute-start(bf16[264,1024]{1,0:T(8,128)(2,1)S(1)} %pad_maximum_fusion.refs_0_), channel_id=1, source_target_pairs={{0,192},{8,200},{16,208},{24,216},{32,224},{40,232},{48,240},{56,2... | collective-permute-start | bytes 1622024 | tf_op jit(solution)/shard_map/ppermute | solution.py:54
  5.4 1.5 %collective-permute-start.11 = (bf16[264,1024]{1,0:T(8,128)(2,1)S(1)}, bf16[264,1024]{1,0:T(8,128)(2,1)S(1)}, u32[]{:S(2)}, u32[]{:S(2)}) collective-permute-start(bf16[264,1024]{1,0:T(8,128)(2,1)S(1)} %pad_maximum_fusion.refs_0_), channel_id=1, source_target_pairs={{0,16},{8,24},{16,32},{24,40},{32,48},{40,56},{48,0},{56,8},{64,80... | collective-permute-start | bytes 1622024 | tf_op jit(solution)/shard_map/ppermute | solution.py:54
  6.9 1.7 %collective-permute-start.13 = (bf16[264,1024]{1,0:T(8,128)(2,1)S(1)}, bf16[264,1024]{1,0:T(8,128)(2,1)S(1)}, u32[]{:S(2)}, u32[]{:S(2)}) collective-permute-start(bf16[264,1024]{1,0:T(8,128)(2,1)S(1)} %pad_maximum_fusion.refs_0_), channel_id=1, source_target_pairs={{0,48},{8,56},{16,0},{24,8},{32,16},{40,24},{48,32},{56,40},{64,11... | collective-permute-start | bytes 1622024 | tf_op jit(solution)/shard_map/ppermute | solution.py:54
  8.6 0.8 collective-permute-start.1
  9.4 7.5 %collective-permute-done.17.refs_18_ = bf16[264,1024]{1,0:T(8,128)(2,1)S(1)} collective-permute-done((bf16[264,1024]{1,0:T(8,128)(2,1)S(1)}, bf16[264,1024]{1,0:T(8,128)(2,1)S(1)}, u32[]{:S(2)}, u32[]{:S(2)}) %collective-permute-start.17) | collective-permute-done | bytes 540704 | tf_op jit(solution)/shard_map/ppermute | solution.py:54
  16.9 1.9 %collective-permute-start = (bf16[264,1024]{1,0:T(8,128)(2,1)S(1)}, bf16[264,1024]{1,0:T(8,128)(2,1)S(1)}, u32[]{:S(2)}, u32[]{:S(2)}) collective-permute-start(bf16[264,1024]{1,0:T(8,128)(2,1)S(1)} %pad_maximum_fusion.refs_0_), channel_id=1, source_target_pairs={{0,1},{1,2},{2,3},{3,4},{4,5},{5,6},{6,7},{7,0},{8,9},{9,10},{10,1... | collective-permute-start | bytes 1622024 | tf_op jit(solution)/shard_map/ppermute | solution.py:62
  18.8 1.5 %collective-permute-done.11.refs_12_ = bf16[264,1024]{1,0:T(8,128)(2,1)S(1)} collective-permute-done((bf16[264,1024]{1,0:T(8,128)(2,1)S(1)}, bf16[264,1024]{1,0:T(8,128)(2,1)S(1)}, u32[]{:S(2)}, u32[]{:S(2)}) %collective-permute-start.11) | collective-permute-done | bytes 540704 | tf_op jit(solution)/shard_map/ppermute | solution.py:54
  20.3 1.2 collective-permute-done.15.refs_16_
  21.5 1.7 %collective-permute-start.21 = (bf16[264,1024]{1,0:T(8,128)(2,1)S(1)}, bf16[264,1024]{1,0:T(8,128)(2,1)S(1)}, u32[]{:S(2)}, u32[]{:S(2)}) collective-permute-start(bf16[264,1024]{1,0:T(8,128)(2,1)S(1)} %collective-permute-done.17.refs_18_), channel_id=1, source_target_pairs={{0,48},{8,56},{16,0},{24,8},{32,16},{40,24},{48,32},{56,40},{64,11... | collective-permute-start | bytes 1622024 | tf_op jit(solution)/shard_map/ppermute | solution.py:54
  23.3 2.1 %collective-permute-start.25 = (bf16[264,1024]{1,0:T(8,128)(2,1)S(1)}, bf16[264,1024]{1,0:T(8,128)(2,1)S(1)}, u32[]{:S(2)}, u32[]{:S(2)}) collective-permute-start(bf16[264,1024]{1,0:T(8,128)(2,1)S(1)} %collective-permute-done.11.refs_12_), channel_id=1, source_target_pairs={{0,192},{8,200},{16,208},{24,216},{32,224},{40,232},{48,240},{56,2... | collective-permute-start | bytes 1622024 | tf_op jit(solution)/shard_map/ppermute | solution.py:54
  25.4 4.7 %collective-permute-done.refs_1_ = bf16[264,1024]{1,0:T(8,128)(2,1)S(1)} collective-permute-done((bf16[264,1024]{1,0:T(8,128)(2,1)S(1)}, bf16[264,1024]{1,0:T(8,128)(2,1)S(1)}, u32[]{:S(2)}, u32[]{:S(2)}) %collective-permute-start) | collective-permute-done | bytes 540704 | tf_op jit(solution)/shard_map/ppermute | solution.py:62
  30.1 1.0 collective-permute-start.23
  31.1 4.2 %collective-permute-start.3 = (bf16[264,1024]{1,0:T(8,128)(2,1)S(1)}, bf16[264,1024]{1,0:T(8,128)(2,1)S(1)}, u32[]{:S(2)}, u32[]{:S(2)}) collective-permute-start(bf16[264,1024]{1,0:T(8,128)(2,1)S(1)} %collective-permute-done.1.refs_2_), channel_id=1, source_target_pairs={{0,7},{1,0},{2,1},{3,2},{4,3},{5,4},{6,5},{7,6},{8,15},{9,8},{10,9... | collective-permute-start | bytes 1622024 | tf_op jit(solution)/shard_map/ppermute | solution.py:62
  35.4 1.6 %collective-permute-start.2 = (bf16[264,1024]{1,0:T(8,128)(2,1)S(1)}, bf16[264,1024]{1,0:T(8,128)(2,1)S(1)}, u32[]{:S(2)}, u32[]{:S(2)}) collective-permute-start(bf16[264,1024]{1,0:T(8,128)(2,1)S(1)} %collective-permute-done.refs_1_), channel_id=1, source_target_pairs={{0,1},{1,2},{2,3},{3,4},{4,5},{5,6},{6,7},{7,0},{8,9},{9,10},{10,1... | collective-permute-start | bytes 1622024 | tf_op jit(solution)/shard_map/ppermute | solution.py:62
  36.9 0.3 collective-permute-done.25.refs_26_
  37.2 0.3 collective-permute-start.27
  37.5 3.4 %collective-permute-done.19.refs_20_ = bf16[264,1024]{1,0:T(8,128)(2,1)S(1)} collective-permute-done((bf16[264,1024]{1,0:T(8,128)(2,1)S(1)}, bf16[264,1024]{1,0:T(8,128)(2,1)S(1)}, u32[]{:S(2)}, u32[]{:S(2)}) %collective-permute-start.19) | collective-permute-done | bytes 540704 | tf_op jit(solution)/shard_map/ppermute | solution.py:54
  41.0 4.2 %collective-permute-done.23.refs_24_ = bf16[264,1024]{1,0:T(8,128)(2,1)S(1)} collective-permute-done((bf16[264,1024]{1,0:T(8,128)(2,1)S(1)}, bf16[264,1024]{1,0:T(8,128)(2,1)S(1)}, u32[]{:S(2)}, u32[]{:S(2)}) %collective-permute-start.23) | collective-permute-done | bytes 540704 | tf_op jit(solution)/shard_map/ppermute | solution.py:54
  45.2 0.5 collective-permute-start.16
  45.7 1.9 %collective-permute-done.2.refs_3_ = bf16[264,1024]{1,0:T(8,128)(2,1)S(1)} collective-permute-done((bf16[264,1024]{1,0:T(8,128)(2,1)S(1)}, bf16[264,1024]{1,0:T(8,128)(2,1)S(1)}, u32[]{:S(2)}, u32[]{:S(2)}) %collective-permute-start.2) | collective-permute-done | bytes 540704 | tf_op jit(solution)/shard_map/ppermute | solution.py:62
  47.7 4.6 %collective-permute-done.27.refs_28_ = bf16[264,1024]{1,0:T(8,128)(2,1)S(1)} collective-permute-done((bf16[264,1024]{1,0:T(8,128)(2,1)S(1)}, bf16[264,1024]{1,0:T(8,128)(2,1)S(1)}, u32[]{:S(2)}, u32[]{:S(2)}) %collective-permute-start.27) | collective-permute-done | bytes 540704 | tf_op jit(solution)/shard_map/ppermute | solution.py:54
  52.3 3.6 %collective-permute-done.31.refs_32_ = bf16[264,1024]{1,0:T(8,128)(2,1)S(1)} collective-permute-done((bf16[264,1024]{1,0:T(8,128)(2,1)S(1)}, bf16[264,1024]{1,0:T(8,128)(2,1)S(1)}, u32[]{:S(2)}, u32[]{:S(2)}) %collective-permute-start.31) | collective-permute-done | bytes 540704 | tf_op jit(solution)/shard_map/ppermute | solution.py:54
  55.9 1.9 %collective-permute-start.4 = (bf16[128,1024]{1,0:T(8,128)(2,1)S(1)}, bf16[128,1024]{1,0:T(8,128)(2,1)S(1)}, u32[]{:S(2)}, u32[]{:S(2)}) collective-permute-start(bf16[128,1024]{1,0:T(8,128)(2,1)S(1)} %slice.16), channel_id=1, source_target_pairs={{0,1},{1,2},{2,3},{3,4},{4,5},{5,6},{6,7},{7,0},{8,9},{9,10},{10,1... | collective-permute-start | bytes 786440 | tf_op jit(solution)/shard_map/ppermute | solution.py:62
  57.8 2.8 %collective-permute-start.29 = (bf16[264,1024]{1,0:T(8,128)(2,1)S(1)}, bf16[264,1024]{1,0:T(8,128)(2,1)}, u32[]{:S(2)}, u32[]{:S(2)}) collective-permute-start(bf16[264,1024]{1,0:T(8,128)(2,1)S(1)} %collective-permute-done.21.refs_22_), channel_id=1, source_target_pairs={{0,48},{8,56},{16,0},{24,8},{32,16},{40,24},{48,32},{56,40},{64,11... | collective-permute-start | bytes 1622024 | tf_op jit(solution)/shard_map/ppermute | solution.py:54
  60.7 0.8 copy-done.19
  61.4 2.7 %collective-permute-start.6 = (bf16[128,1024]{1,0:T(8,128)(2,1)S(1)}, bf16[128,1024]{1,0:T(8,128)(2,1)S(1)}, u32[]{:S(2)}, u32[]{:S(2)}) collective-permute-start(bf16[128,1024]{1,0:T(8,128)(2,1)S(1)} %slice.18), channel_id=1, source_target_pairs={{0,7},{1,0},{2,1},{3,2},{4,3},{5,4},{6,5},{7,6},{8,15},{9,8},{10,9... | collective-permute-start | bytes 786440 | tf_op jit(solution)/shard_map/ppermute | solution.py:62
  64.2 3.2 %collective-permute-start.7 = (bf16[136,1024]{1,0:T(8,128)(2,1)S(1)}, bf16[136,1024]{1,0:T(8,128)(2,1)S(1)}, u32[]{:S(2)}, u32[]{:S(2)}) collective-permute-start(bf16[136,1024]{1,0:T(8,128)(2,1)S(1)} %slice.19), channel_id=1, source_target_pairs={{0,7},{1,0},{2,1},{3,2},{4,3},{5,4},{6,5},{7,6},{8,15},{9,8},{10,9... | collective-permute-start | bytes 835592 | tf_op jit(solution)/shard_map/ppermute | solution.py:62
  67.4 1.8 %collective-permute-start.33 = (bf16[264,1024]{1,0:T(8,128)(2,1)S(1)}, bf16[264,1024]{1,0:T(8,128)(2,1)}, u32[]{:S(2)}, u32[]{:S(2)}) collective-permute-start(bf16[264,1024]{1,0:T(8,128)(2,1)S(1)} %collective-permute-done.25.refs_26_), channel_id=1, source_target_pairs={{0,192},{8,200},{16,208},{24,216},{32,224},{40,232},{48,240},{56,2... | collective-permute-start | bytes 1622024 | tf_op jit(solution)/shard_map/ppermute | solution.py:54
  69.3 1.2 collective-permute-done.6.refs_7_
  70.5 3.6 %collective-permute-start.8 = (bf16[128,1024]{1,0:T(8,128)(2,1)S(1)}, bf16[128,1024]{1,0:T(8,128)(2,1)S(1)}, u32[]{:S(2)}, u32[]{:S(2)}) collective-permute-start(bf16[128,1024]{1,0:T(8,128)(2,1)S(1)} %collective-permute-done.4.refs_5_), channel_id=1, source_target_pairs={{0,1},{1,2},{2,3},{3,4},{4,5},{5,6},{6,7},{7,0},{8,9},{9,10},{10,1... | collective-permute-start | bytes 786440 | tf_op jit(solution)/shard_map/ppermute | solution.py:62
  74.1 1.4 collective-permute-done.5.refs_6_
  75.5 2.8 %collective-permute-done.8.refs_9_ = bf16[128,1024]{1,0:T(8,128)(2,1)S(1)} collective-permute-done((bf16[128,1024]{1,0:T(8,128)(2,1)S(1)}, bf16[128,1024]{1,0:T(8,128)(2,1)S(1)}, u32[]{:S(2)}, u32[]{:S(2)}) %collective-permute-start.8) | collective-permute-done | bytes 262176 | tf_op jit(solution)/shard_map/ppermute | solution.py:62
  78.3 0.5 collective-permute-start.26
  78.9 6.6 %collective-permute-done.35.refs_36_ = bf16[264,1024]{1,0:T(8,128)(2,1)} collective-permute-done((bf16[264,1024]{1,0:T(8,128)(2,1)S(1)}, bf16[264,1024]{1,0:T(8,128)(2,1)}, u32[]{:S(2)}, u32[]{:S(2)}) %collective-permute-start.35) | collective-permute-done | bytes 540704 | tf_op jit(solution)/shard_map/ppermute | solution.py:54
  85.5 0.6 collective-permute-done.37.refs_38_
  86.2 0.5 collective-permute-start.32
  86.7 1.7 %collective-permute-start.39 = (bf16[264,1024]{1,0:T(8,128)(2,1)}, bf16[264,1024]{1,0:T(8,128)(2,1)}, u32[]{:S(2)}, u32[]{:S(2)}) collective-permute-start(bf16[264,1024]{1,0:T(8,128)(2,1)} %collective-permute-done.29.refs_30_), channel_id=1, source_target_pairs={{0,192},{8,200},{16,208},{24,216},{32,224},{40,232},{48,240},{56,2... | collective-permute-start | bytes 1622024 | tf_op jit(solution)/shard_map/ppermute | solution.py:54
  88.4 1.8 %collective-permute-start.9 = (bf16[136,1024]{1,0:T(8,128)(2,1)S(1)}, bf16[136,1024]{1,0:T(8,128)(2,1)S(1)}, u32[]{:S(2)}, u32[]{:S(2)}) collective-permute-start(bf16[136,1024]{1,0:T(8,128)(2,1)S(1)} %collective-permute-done.7.refs_8_), channel_id=1, source_target_pairs={{0,7},{1,0},{2,1},{3,2},{4,3},{5,4},{6,5},{7,6},{8,15},{9,8},{10,9... | collective-permute-start | bytes 835592 | tf_op jit(solution)/shard_map/ppermute | solution.py:62
  90.4 0.6 collective-permute-start.34
  91.1 6.9 %collective-permute-done.9.refs_10_ = bf16[136,1024]{1,0:T(8,128)(2,1)S(1)} collective-permute-done((bf16[136,1024]{1,0:T(8,128)(2,1)S(1)}, bf16[136,1024]{1,0:T(8,128)(2,1)S(1)}, u32[]{:S(2)}, u32[]{:S(2)}) %collective-permute-start.9) | collective-permute-done | bytes 278560 | tf_op jit(solution)/shard_map/ppermute | solution.py:62
  98.0 3.5 %collective-permute-done.39.refs_40_ = bf16[264,1024]{1,0:T(8,128)(2,1)} collective-permute-done((bf16[264,1024]{1,0:T(8,128)(2,1)}, bf16[264,1024]{1,0:T(8,128)(2,1)}, u32[]{:S(2)}, u32[]{:S(2)}) %collective-permute-start.39) | collective-permute-done | bytes 540704 | tf_op jit(solution)/shard_map/ppermute | solution.py:54
  101.6 0.6 pad_add_fusion.where_ref
  102.3 1.5 %collective-permute-done.40.refs_41_ = bf16[264,1024]{1,0:T(8,128)(2,1)} collective-permute-done((bf16[264,1024]{1,0:T(8,128)(2,1)}, bf16[264,1024]{1,0:T(8,128)(2,1)}, u32[]{:S(2)}, u32[]{:S(2)}) %collective-permute-start.40) | collective-permute-done | bytes 540704 | tf_op jit(solution)/shard_map/ppermute | solution.py:58
  103.8 19.8 %compare.36 = f32[8,1,256]{2,1,0:T(1,128)} custom-call(s32[2]{0:T(128)} %pad_add_fusion.where_ref, s32[32,32]{1,0:T(8,128)} %pattern_ref.1, bf16[264,1024]{1,0:T(8,128)(2,1)} %copy-done.1, bf16[264,1024]{1,0:T(8,128)(2,1)} %copy-done.10, bf16[264,1024]{1,0:T(8,128)(2,1)} %copy-done.9, bf16[264,1024]{1,0:T(8,128)(2,1)} %copy-done.3, ...), custom_call_target="tpu_custom_call" | custom-call | flops 8589934592 | bytes 20971520 | tf_op jit(solution)/shard_map/compare/pallas_call | solution.py:281
  123.7 14.2 %all_to_all.5 = f32[8,1,256]{2,1,0:T(1,128)S(1)} all-to-all(f32[8,1,256]{2,1,0:T(1,128)} %compare.36), channel_id=1, replica_groups=mesh['grp'=32,'own'=8] {'own'}, dimensions={0} | all-to-all | bytes 16384 | tf_op jit(solution)/shard_map/all_to_all | solution.py:359
  137.8 0.7 reshape.28
  (123 shorter events, 1.1 us)
Async XLA Ops:
  2.3 61.8 %copy-start.1 = (bf16[264,1024]{1,0:T(8,128)(2,1)}, bf16[264,1024]{1,0:T(8,128)(2,1)S(1)}, u32[]{:S(2)}) copy-start(bf16[264,1024]{1,0:T(8,128)(2,1)S(1)} %pad_maximum_fusion.refs_0_) | copy-start | bytes 1622020
  2.3 14.6 %collective-permute-start.17 = (bf16[264,1024]{1,0:T(8,128)(2,1)S(1)}, bf16[264,1024]{1,0:T(8,128)(2,1)S(1)}, u32[]{:S(2)}, u32[]{:S(2)}) collective-permute-start(bf16[264,1024]{1,0:T(8,128)(2,1)S(1)} %pad_maximum_fusion.refs_0_), channel_id=1, source_target_pairs={{0,192},{8,200},{16,208},{24,216},{32,224},{40,232},{48,240},{56,2... | collective-permute-start | bytes 1622024 | tf_op jit(solution)/shard_map/ppermute | solution.py:54
  5.4 14.9 %collective-permute-start.11 = (bf16[264,1024]{1,0:T(8,128)(2,1)S(1)}, bf16[264,1024]{1,0:T(8,128)(2,1)S(1)}, u32[]{:S(2)}, u32[]{:S(2)}) collective-permute-start(bf16[264,1024]{1,0:T(8,128)(2,1)S(1)} %pad_maximum_fusion.refs_0_), channel_id=1, source_target_pairs={{0,16},{8,24},{16,32},{24,40},{32,48},{40,56},{48,0},{56,8},{64,80... | collective-permute-start | bytes 1622024 | tf_op jit(solution)/shard_map/ppermute | solution.py:54
  6.9 14.7 %collective-permute-start.15 = (bf16[264,1024]{1,0:T(8,128)(2,1)S(1)}, bf16[264,1024]{1,0:T(8,128)(2,1)S(1)}, u32[]{:S(2)}, u32[]{:S(2)}) collective-permute-start(bf16[264,1024]{1,0:T(8,128)(2,1)S(1)} %pad_maximum_fusion.refs_0_), channel_id=1, source_target_pairs={{0,64},{8,72},{16,80},{24,88},{32,96},{40,104},{48,112},{56,120},{... | collective-permute-start | bytes 1622024 | tf_op jit(solution)/shard_map/ppermute | solution.py:54
  6.9 16.4 %collective-permute-start.13 = (bf16[264,1024]{1,0:T(8,128)(2,1)S(1)}, bf16[264,1024]{1,0:T(8,128)(2,1)S(1)}, u32[]{:S(2)}, u32[]{:S(2)}) collective-permute-start(bf16[264,1024]{1,0:T(8,128)(2,1)S(1)} %pad_maximum_fusion.refs_0_), channel_id=1, source_target_pairs={{0,48},{8,56},{16,0},{24,8},{32,16},{40,24},{48,32},{56,40},{64,11... | collective-permute-start | bytes 1622024 | tf_op jit(solution)/shard_map/ppermute | solution.py:54
  8.6 16.8 %collective-permute-start.1 = (bf16[264,1024]{1,0:T(8,128)(2,1)S(1)}, bf16[264,1024]{1,0:T(8,128)(2,1)S(1)}, u32[]{:S(2)}, u32[]{:S(2)}) collective-permute-start(bf16[264,1024]{1,0:T(8,128)(2,1)S(1)} %pad_maximum_fusion.refs_0_), channel_id=1, source_target_pairs={{0,7},{1,0},{2,1},{3,2},{4,3},{5,4},{6,5},{7,6},{8,15},{9,8},{10,9... | collective-permute-start | bytes 1622024 | tf_op jit(solution)/shard_map/ppermute | solution.py:62
  16.9 86.9 %copy-start.5 = (bf16[264,1024]{1,0:T(8,128)(2,1)}, bf16[264,1024]{1,0:T(8,128)(2,1)S(1)}, u32[]{:S(2)}) copy-start(bf16[264,1024]{1,0:T(8,128)(2,1)S(1)} %collective-permute-done.17.refs_18_) | copy-start | bytes 1622020
  16.9 13.2 %collective-permute-start = (bf16[264,1024]{1,0:T(8,128)(2,1)S(1)}, bf16[264,1024]{1,0:T(8,128)(2,1)S(1)}, u32[]{:S(2)}, u32[]{:S(2)}) collective-permute-start(bf16[264,1024]{1,0:T(8,128)(2,1)S(1)} %pad_maximum_fusion.refs_0_), channel_id=1, source_target_pairs={{0,1},{1,2},{2,3},{3,4},{4,5},{5,6},{6,7},{7,0},{8,9},{9,10},{10,1... | collective-permute-start | bytes 1622024 | tf_op jit(solution)/shard_map/ppermute | solution.py:62
  20.3 83.5 %copy-start.6 = (bf16[264,1024]{1,0:T(8,128)(2,1)}, bf16[264,1024]{1,0:T(8,128)(2,1)S(1)}, u32[]{:S(2)}) copy-start(bf16[264,1024]{1,0:T(8,128)(2,1)S(1)} %collective-permute-done.11.refs_12_) | copy-start | bytes 1622020
  20.3 10.8 %collective-permute-start.10 = (bf16[264,1024]{1,0:T(8,128)(2,1)S(1)}, bf16[264,1024]{1,0:T(8,128)(2,1)S(1)}, u32[]{:S(2)}, u32[]{:S(2)}) collective-permute-start(bf16[264,1024]{1,0:T(8,128)(2,1)S(1)} %pad_maximum_fusion.refs_0_), channel_id=1, source_target_pairs={{0,8},{8,0},{16,24},{24,16},{32,40},{40,32},{48,56},{56,48},{64,72... | collective-permute-start | bytes 1622024 | tf_op jit(solution)/shard_map/ppermute | solution.py:58
  21.5 82.3 %copy-start.7 = (bf16[264,1024]{1,0:T(8,128)(2,1)}, bf16[264,1024]{1,0:T(8,128)(2,1)S(1)}, u32[]{:S(2)}) copy-start(bf16[264,1024]{1,0:T(8,128)(2,1)S(1)} %collective-permute-done.15.refs_16_) | copy-start | bytes 1622020
  21.5 13.8 %collective-permute-start.21 = (bf16[264,1024]{1,0:T(8,128)(2,1)S(1)}, bf16[264,1024]{1,0:T(8,128)(2,1)S(1)}, u32[]{:S(2)}, u32[]{:S(2)}) collective-permute-start(bf16[264,1024]{1,0:T(8,128)(2,1)S(1)} %collective-permute-done.17.refs_18_), channel_id=1, source_target_pairs={{0,48},{8,56},{16,0},{24,8},{32,16},{40,24},{48,32},{56,40},{64,11... | collective-permute-start | bytes 1622024 | tf_op jit(solution)/shard_map/ppermute | solution.py:54
  23.3 80.5 %copy-start.8 = (bf16[264,1024]{1,0:T(8,128)(2,1)}, bf16[264,1024]{1,0:T(8,128)(2,1)S(1)}, u32[]{:S(2)}) copy-start(bf16[264,1024]{1,0:T(8,128)(2,1)S(1)} %collective-permute-done.13.refs_14_) | copy-start | bytes 1622020
  23.3 13.9 %collective-permute-start.25 = (bf16[264,1024]{1,0:T(8,128)(2,1)S(1)}, bf16[264,1024]{1,0:T(8,128)(2,1)S(1)}, u32[]{:S(2)}, u32[]{:S(2)}) collective-permute-start(bf16[264,1024]{1,0:T(8,128)(2,1)S(1)} %collective-permute-done.11.refs_12_), channel_id=1, source_target_pairs={{0,192},{8,200},{16,208},{24,216},{32,224},{40,232},{48,240},{56,2... | collective-permute-start | bytes 1622024 | tf_op jit(solution)/shard_map/ppermute | solution.py:54
  25.4 78.4 %copy-start.9 = (bf16[264,1024]{1,0:T(8,128)(2,1)}, bf16[264,1024]{1,0:T(8,128)(2,1)S(1)}, u32[]{:S(2)}) copy-start(bf16[264,1024]{1,0:T(8,128)(2,1)S(1)} %collective-permute-done.1.refs_2_) | copy-start | bytes 1622020
  25.4 15.6 %collective-permute-start.19 = (bf16[264,1024]{1,0:T(8,128)(2,1)S(1)}, bf16[264,1024]{1,0:T(8,128)(2,1)S(1)}, u32[]{:S(2)}, u32[]{:S(2)}) collective-permute-start(bf16[264,1024]{1,0:T(8,128)(2,1)S(1)} %collective-permute-done.15.refs_16_), channel_id=1, source_target_pairs={{0,16},{8,24},{16,32},{24,40},{32,48},{40,56},{48,0},{56,8},{64,80... | collective-permute-start | bytes 1622024 | tf_op jit(solution)/shard_map/ppermute | solution.py:54
  30.1 15.1 %collective-permute-start.23 = (bf16[264,1024]{1,0:T(8,128)(2,1)S(1)}, bf16[264,1024]{1,0:T(8,128)(2,1)S(1)}, u32[]{:S(2)}, u32[]{:S(2)}) collective-permute-start(bf16[264,1024]{1,0:T(8,128)(2,1)S(1)} %collective-permute-done.13.refs_14_), channel_id=1, source_target_pairs={{0,64},{8,72},{16,80},{24,88},{32,96},{40,104},{48,112},{56,120},{... | collective-permute-start | bytes 1622024 | tf_op jit(solution)/shard_map/ppermute | solution.py:54
  31.1 14.1 %collective-permute-start.3 = (bf16[264,1024]{1,0:T(8,128)(2,1)S(1)}, bf16[264,1024]{1,0:T(8,128)(2,1)S(1)}, u32[]{:S(2)}, u32[]{:S(2)}) collective-permute-start(bf16[264,1024]{1,0:T(8,128)(2,1)S(1)} %collective-permute-done.1.refs_2_), channel_id=1, source_target_pairs={{0,7},{1,0},{2,1},{3,2},{4,3},{5,4},{6,5},{7,6},{8,15},{9,8},{10,9... | collective-permute-start | bytes 1622024 | tf_op jit(solution)/shard_map/ppermute | solution.py:62
  35.4 12.3 %collective-permute-start.2 = (bf16[264,1024]{1,0:T(8,128)(2,1)S(1)}, bf16[264,1024]{1,0:T(8,128)(2,1)S(1)}, u32[]{:S(2)}, u32[]{:S(2)}) collective-permute-start(bf16[264,1024]{1,0:T(8,128)(2,1)S(1)} %collective-permute-done.refs_1_), channel_id=1, source_target_pairs={{0,1},{1,2},{2,3},{3,4},{4,5},{5,6},{6,7},{7,0},{8,9},{9,10},{10,1... | collective-permute-start | bytes 1622024 | tf_op jit(solution)/shard_map/ppermute | solution.py:62
  37.2 15.0 %collective-permute-start.27 = (bf16[264,1024]{1,0:T(8,128)(2,1)S(1)}, bf16[264,1024]{1,0:T(8,128)(2,1)S(1)}, u32[]{:S(2)}, u32[]{:S(2)}) collective-permute-start(bf16[264,1024]{1,0:T(8,128)(2,1)S(1)} %collective-permute-done.11.refs_12_), channel_id=1, source_target_pairs={{0,16},{8,24},{16,32},{24,40},{32,48},{40,56},{48,0},{56,8},{64,80... | collective-permute-start | bytes 1622024 | tf_op jit(solution)/shard_map/ppermute | solution.py:54
  41.0 14.9 %collective-permute-start.31 = (bf16[264,1024]{1,0:T(8,128)(2,1)S(1)}, bf16[264,1024]{1,0:T(8,128)(2,1)S(1)}, u32[]{:S(2)}, u32[]{:S(2)}) collective-permute-start(bf16[264,1024]{1,0:T(8,128)(2,1)S(1)} %collective-permute-done.15.refs_16_), channel_id=1, source_target_pairs={{0,64},{8,72},{16,80},{24,88},{32,96},{40,104},{48,112},{56,120},{... | collective-permute-start | bytes 1622024 | tf_op jit(solution)/shard_map/ppermute | solution.py:54
  45.2 12.6 %collective-permute-start.12 = (bf16[264,1024]{1,0:T(8,128)(2,1)S(1)}, bf16[264,1024]{1,0:T(8,128)(2,1)S(1)}, u32[]{:S(2)}, u32[]{:S(2)}) collective-permute-start(bf16[264,1024]{1,0:T(8,128)(2,1)S(1)} %collective-permute-done.11.refs_12_), channel_id=1, source_target_pairs={{0,8},{8,0},{16,24},{24,16},{32,40},{40,32},{48,56},{56,48},{64,72... | collective-permute-start | bytes 1622024 | tf_op jit(solution)/shard_map/ppermute | solution.py:58
  45.2 15.4 %collective-permute-start.16 = (bf16[264,1024]{1,0:T(8,128)(2,1)S(1)}, bf16[264,1024]{1,0:T(8,128)(2,1)S(1)}, u32[]{:S(2)}, u32[]{:S(2)}) collective-permute-start(bf16[264,1024]{1,0:T(8,128)(2,1)S(1)} %collective-permute-done.15.refs_16_), channel_id=1, source_target_pairs={{0,8},{8,0},{16,24},{24,16},{32,40},{40,32},{48,56},{56,48},{64,72... | collective-permute-start | bytes 1622024 | tf_op jit(solution)/shard_map/ppermute | solution.py:58
  47.7 56.2 %copy-start.3 = (bf16[264,1024]{1,0:T(8,128)(2,1)}, bf16[264,1024]{1,0:T(8,128)(2,1)S(1)}, u32[]{:S(2)}) copy-start(bf16[264,1024]{1,0:T(8,128)(2,1)S(1)} %collective-permute-done.2.refs_3_) | copy-start | bytes 1622020
  47.7 16.5 %collective-permute-start.14 = (bf16[264,1024]{1,0:T(8,128)(2,1)S(1)}, bf16[264,1024]{1,0:T(8,128)(2,1)S(1)}, u32[]{:S(2)}, u32[]{:S(2)}) collective-permute-start(bf16[264,1024]{1,0:T(8,128)(2,1)S(1)} %collective-permute-done.13.refs_14_), channel_id=1, source_target_pairs={{0,8},{8,0},{16,24},{24,16},{32,40},{40,32},{48,56},{56,48},{64,72... | collective-permute-start | bytes 1622024 | tf_op jit(solution)/shard_map/ppermute | solution.py:58
  52.2 15.2 %collective-permute-start.18 = (bf16[264,1024]{1,0:T(8,128)(2,1)S(1)}, bf16[264,1024]{1,0:T(8,128)(2,1)S(1)}, u32[]{:S(2)}, u32[]{:S(2)}) collective-permute-start(bf16[264,1024]{1,0:T(8,128)(2,1)S(1)} %collective-permute-done.17.refs_18_), channel_id=1, source_target_pairs={{0,8},{8,0},{16,24},{24,16},{32,40},{40,32},{48,56},{56,48},{64,72... | collective-permute-start | bytes 1622024 | tf_op jit(solution)/shard_map/ppermute | solution.py:58
  55.9 11.5 %collective-permute-start.4 = (bf16[128,1024]{1,0:T(8,128)(2,1)S(1)}, bf16[128,1024]{1,0:T(8,128)(2,1)S(1)}, u32[]{:S(2)}, u32[]{:S(2)}) collective-permute-start(bf16[128,1024]{1,0:T(8,128)(2,1)S(1)} %slice.16), channel_id=1, source_target_pairs={{0,1},{1,2},{2,3},{3,4},{4,5},{5,6},{6,7},{7,0},{8,9},{9,10},{10,1... | collective-permute-start | bytes 786440 | tf_op jit(solution)/shard_map/ppermute | solution.py:62
  57.8 20.5 %collective-permute-start.29 = (bf16[264,1024]{1,0:T(8,128)(2,1)S(1)}, bf16[264,1024]{1,0:T(8,128)(2,1)}, u32[]{:S(2)}, u32[]{:S(2)}) collective-permute-start(bf16[264,1024]{1,0:T(8,128)(2,1)S(1)} %collective-permute-done.21.refs_22_), channel_id=1, source_target_pairs={{0,48},{8,56},{16,0},{24,8},{32,16},{40,24},{48,32},{56,40},{64,11... | collective-permute-start | bytes 1622024 | tf_op jit(solution)/shard_map/ppermute | solution.py:54
  61.4 9.1 %collective-permute-start.6 = (bf16[128,1024]{1,0:T(8,128)(2,1)S(1)}, bf16[128,1024]{1,0:T(8,128)(2,1)S(1)}, u32[]{:S(2)}, u32[]{:S(2)}) collective-permute-start(bf16[128,1024]{1,0:T(8,128)(2,1)S(1)} %slice.18), channel_id=1, source_target_pairs={{0,7},{1,0},{2,1},{3,2},{4,3},{5,4},{6,5},{7,6},{8,15},{9,8},{10,9... | collective-permute-start | bytes 786440 | tf_op jit(solution)/shard_map/ppermute | solution.py:62
  64.2 9.9 %collective-permute-start.7 = (bf16[136,1024]{1,0:T(8,128)(2,1)S(1)}, bf16[136,1024]{1,0:T(8,128)(2,1)S(1)}, u32[]{:S(2)}, u32[]{:S(2)}) collective-permute-start(bf16[136,1024]{1,0:T(8,128)(2,1)S(1)} %slice.19), channel_id=1, source_target_pairs={{0,7},{1,0},{2,1},{3,2},{4,3},{5,4},{6,5},{7,6},{8,15},{9,8},{10,9... | collective-permute-start | bytes 835592 | tf_op jit(solution)/shard_map/ppermute | solution.py:62
  67.4 8.1 %collective-permute-start.5 = (bf16[136,1024]{1,0:T(8,128)(2,1)S(1)}, bf16[136,1024]{1,0:T(8,128)(2,1)S(1)}, u32[]{:S(2)}, u32[]{:S(2)}) collective-permute-start(bf16[136,1024]{1,0:T(8,128)(2,1)S(1)} %slice.17), channel_id=1, source_target_pairs={{0,1},{1,2},{2,3},{3,4},{4,5},{5,6},{6,7},{7,0},{8,9},{9,10},{10,1... | collective-permute-start | bytes 835592 | tf_op jit(solution)/shard_map/ppermute | solution.py:62
  67.4 11.4 %collective-permute-start.33 = (bf16[264,1024]{1,0:T(8,128)(2,1)S(1)}, bf16[264,1024]{1,0:T(8,128)(2,1)}, u32[]{:S(2)}, u32[]{:S(2)}) collective-permute-start(bf16[264,1024]{1,0:T(8,128)(2,1)S(1)} %collective-permute-done.25.refs_26_), channel_id=1, source_target_pairs={{0,192},{8,200},{16,208},{24,216},{32,224},{40,232},{48,240},{56,2... | collective-permute-start | bytes 1622024 | tf_op jit(solution)/shard_map/ppermute | solution.py:54
  70.5 7.8 %collective-permute-start.8 = (bf16[128,1024]{1,0:T(8,128)(2,1)S(1)}, bf16[128,1024]{1,0:T(8,128)(2,1)S(1)}, u32[]{:S(2)}, u32[]{:S(2)}) collective-permute-start(bf16[128,1024]{1,0:T(8,128)(2,1)S(1)} %collective-permute-done.4.refs_5_), channel_id=1, source_target_pairs={{0,1},{1,2},{2,3},{3,4},{4,5},{5,6},{6,7},{7,0},{8,9},{9,10},{10,1... | collective-permute-start | bytes 786440 | tf_op jit(solution)/shard_map/ppermute | solution.py:62
  74.1 11.4 %collective-permute-start.35 = (bf16[264,1024]{1,0:T(8,128)(2,1)S(1)}, bf16[264,1024]{1,0:T(8,128)(2,1)}, u32[]{:S(2)}, u32[]{:S(2)}) collective-permute-start(bf16[264,1024]{1,0:T(8,128)(2,1)S(1)} %collective-permute-done.19.refs_20_), channel_id=1, source_target_pairs={{0,16},{8,24},{16,32},{24,40},{32,48},{40,56},{48,0},{56,8},{64,80... | collective-permute-start | bytes 1622024 | tf_op jit(solution)/shard_map/ppermute | solution.py:54
  75.5 10.7 %collective-permute-start.37 = (bf16[264,1024]{1,0:T(8,128)(2,1)S(1)}, bf16[264,1024]{1,0:T(8,128)(2,1)}, u32[]{:S(2)}, u32[]{:S(2)}) collective-permute-start(bf16[264,1024]{1,0:T(8,128)(2,1)S(1)} %collective-permute-done.23.refs_24_), channel_id=1, source_target_pairs={{0,64},{8,72},{16,80},{24,88},{32,96},{40,104},{48,112},{56,120},{... | collective-permute-start | bytes 1622024 | tf_op jit(solution)/shard_map/ppermute | solution.py:54
  78.3 7.9 %collective-permute-start.20 = (bf16[264,1024]{1,0:T(8,128)(2,1)S(1)}, bf16[264,1024]{1,0:T(8,128)(2,1)S(1)}, u32[]{:S(2)}, u32[]{:S(2)}) collective-permute-start(bf16[264,1024]{1,0:T(8,128)(2,1)S(1)} %collective-permute-done.19.refs_20_), channel_id=1, source_target_pairs={{0,8},{8,0},{16,24},{24,16},{32,40},{40,32},{48,56},{56,48},{64,72... | collective-permute-start | bytes 1622024 | tf_op jit(solution)/shard_map/ppermute | solution.py:58
  78.3 8.4 %collective-permute-start.26 = (bf16[264,1024]{1,0:T(8,128)(2,1)S(1)}, bf16[264,1024]{1,0:T(8,128)(2,1)S(1)}, u32[]{:S(2)}, u32[]{:S(2)}) collective-permute-start(bf16[264,1024]{1,0:T(8,128)(2,1)S(1)} %collective-permute-done.25.refs_26_), channel_id=1, source_target_pairs={{0,8},{8,0},{16,24},{24,16},{32,40},{40,32},{48,56},{56,48},{64,72... | collective-permute-start | bytes 1622024 | tf_op jit(solution)/shard_map/ppermute | solution.py:58
  78.8 9.6 %collective-permute-start.22 = (bf16[264,1024]{1,0:T(8,128)(2,1)S(1)}, bf16[264,1024]{1,0:T(8,128)(2,1)S(1)}, u32[]{:S(2)}, u32[]{:S(2)}) collective-permute-start(bf16[264,1024]{1,0:T(8,128)(2,1)S(1)} %collective-permute-done.21.refs_22_), channel_id=1, source_target_pairs={{0,8},{8,0},{16,24},{24,16},{32,40},{40,32},{48,56},{56,48},{64,72... | collective-permute-start | bytes 1622024 | tf_op jit(solution)/shard_map/ppermute | solution.py:58
  85.5 4.7 %collective-permute-start.24 = (bf16[264,1024]{1,0:T(8,128)(2,1)S(1)}, bf16[264,1024]{1,0:T(8,128)(2,1)S(1)}, u32[]{:S(2)}, u32[]{:S(2)}) collective-permute-start(bf16[264,1024]{1,0:T(8,128)(2,1)S(1)} %collective-permute-done.23.refs_24_), channel_id=1, source_target_pairs={{0,8},{8,0},{16,24},{24,16},{32,40},{40,32},{48,56},{56,48},{64,72... | collective-permute-start | bytes 1622024 | tf_op jit(solution)/shard_map/ppermute | solution.py:58
  86.2 4.2 %collective-permute-start.28 = (bf16[264,1024]{1,0:T(8,128)(2,1)S(1)}, bf16[264,1024]{1,0:T(8,128)(2,1)S(1)}, u32[]{:S(2)}, u32[]{:S(2)}) collective-permute-start(bf16[264,1024]{1,0:T(8,128)(2,1)S(1)} %collective-permute-done.27.refs_28_), channel_id=1, source_target_pairs={{0,8},{8,0},{16,24},{24,16},{32,40},{40,32},{48,56},{56,48},{64,72... | collective-permute-start | bytes 1622024 | tf_op jit(solution)/shard_map/ppermute | solution.py:58
  86.2 4.8 %collective-permute-start.32 = (bf16[264,1024]{1,0:T(8,128)(2,1)S(1)}, bf16[264,1024]{1,0:T(8,128)(2,1)S(1)}, u32[]{:S(2)}, u32[]{:S(2)}) collective-permute-start(bf16[264,1024]{1,0:T(8,128)(2,1)S(1)} %collective-permute-done.31.refs_32_), channel_id=1, source_target_pairs={{0,8},{8,0},{16,24},{24,16},{32,40},{40,32},{48,56},{56,48},{64,72... | collective-permute-start | bytes 1622024 | tf_op jit(solution)/shard_map/ppermute | solution.py:58
  86.7 14.8 %collective-permute-start.39 = (bf16[264,1024]{1,0:T(8,128)(2,1)}, bf16[264,1024]{1,0:T(8,128)(2,1)}, u32[]{:S(2)}, u32[]{:S(2)}) collective-permute-start(bf16[264,1024]{1,0:T(8,128)(2,1)} %collective-permute-done.29.refs_30_), channel_id=1, source_target_pairs={{0,192},{8,200},{16,208},{24,216},{32,224},{40,232},{48,240},{56,2... | collective-permute-start | bytes 1622024 | tf_op jit(solution)/shard_map/ppermute | solution.py:54
  88.4 9.5 %collective-permute-start.9 = (bf16[136,1024]{1,0:T(8,128)(2,1)S(1)}, bf16[136,1024]{1,0:T(8,128)(2,1)S(1)}, u32[]{:S(2)}, u32[]{:S(2)}) collective-permute-start(bf16[136,1024]{1,0:T(8,128)(2,1)S(1)} %collective-permute-done.7.refs_8_), channel_id=1, source_target_pairs={{0,7},{1,0},{2,1},{3,2},{4,3},{5,4},{6,5},{7,6},{8,15},{9,8},{10,9... | collective-permute-start | bytes 835592 | tf_op jit(solution)/shard_map/ppermute | solution.py:62
  90.3 12.0 %collective-permute-start.30 = (bf16[264,1024]{1,0:T(8,128)(2,1)}, bf16[264,1024]{1,0:T(8,128)(2,1)}, u32[]{:S(2)}, u32[]{:S(2)}) collective-permute-start(bf16[264,1024]{1,0:T(8,128)(2,1)} %collective-permute-done.29.refs_30_), channel_id=1, source_target_pairs={{0,8},{8,0},{16,24},{24,16},{32,40},{40,32},{48,56},{56,48},{64,72... | collective-permute-start | bytes 1622024 | tf_op jit(solution)/shard_map/ppermute | solution.py:58
  90.4 11.9 %collective-permute-start.34 = (bf16[264,1024]{1,0:T(8,128)(2,1)}, bf16[264,1024]{1,0:T(8,128)(2,1)}, u32[]{:S(2)}, u32[]{:S(2)}) collective-permute-start(bf16[264,1024]{1,0:T(8,128)(2,1)} %collective-permute-done.33.refs_34_), channel_id=1, source_target_pairs={{0,8},{8,0},{16,24},{24,16},{32,40},{40,32},{48,56},{56,48},{64,72... | collective-permute-start | bytes 1622024 | tf_op jit(solution)/shard_map/ppermute | solution.py:58
  91.0 11.3 %collective-permute-start.36 = (bf16[264,1024]{1,0:T(8,128)(2,1)}, bf16[264,1024]{1,0:T(8,128)(2,1)}, u32[]{:S(2)}, u32[]{:S(2)}) collective-permute-start(bf16[264,1024]{1,0:T(8,128)(2,1)} %collective-permute-done.35.refs_36_), channel_id=1, source_target_pairs={{0,8},{8,0},{16,24},{24,16},{32,40},{40,32},{48,56},{56,48},{64,72... | collective-permute-start | bytes 1622024 | tf_op jit(solution)/shard_map/ppermute | solution.py:58
  98.0 4.3 %collective-permute-start.38 = (bf16[264,1024]{1,0:T(8,128)(2,1)}, bf16[264,1024]{1,0:T(8,128)(2,1)}, u32[]{:S(2)}, u32[]{:S(2)}) collective-permute-start(bf16[264,1024]{1,0:T(8,128)(2,1)} %collective-permute-done.37.refs_38_), channel_id=1, source_target_pairs={{0,8},{8,0},{16,24},{24,16},{32,40},{40,32},{48,56},{56,48},{64,72... | collective-permute-start | bytes 1622024 | tf_op jit(solution)/shard_map/ppermute | solution.py:58
  101.5 2.3 %collective-permute-start.40 = (bf16[264,1024]{1,0:T(8,128)(2,1)}, bf16[264,1024]{1,0:T(8,128)(2,1)}, u32[]{:S(2)}, u32[]{:S(2)}) collective-permute-start(bf16[264,1024]{1,0:T(8,128)(2,1)} %collective-permute-done.39.refs_40_), channel_id=1, source_target_pairs={{0,8},{8,0},{16,24},{24,16},{32,40},{40,32},{48,56},{56,48},{64,72... | collective-permute-start | bytes 1622024 | tf_op jit(solution)/shard_map/ppermute | solution.py:58
  (28 other events, 580.7 us)

commit v2 on v1

--- a/solution.py
+++ b/solution.py
@@ -327,24 +327,16 @@
     up, down = [shard], [shard]
     arrays = [shard]
     queries = [(0, 0, 0)]
-    last, half = n_own // 2, ROWS // 2
-    for hop in range(1, last - 1):
+    for hop in range(1, n_own // 2):
         up.append(along(up[-1], 1, n_own))
         down.append(along(down[-1], -1, n_own))
         at = len(arrays)
         queries += [(at, at, hop), (at + 1, at + 1, -hop)]
         arrays += [up[-1], down[-1]]
-    up_low = along(up[-1][:half], 1, n_own)
-    down_high = along(down[-1][half:], -1, n_own)
-    up_high = along(up[-1][half:], 1, n_own)
-    down_low = along(down[-1][:half], -1, n_own)
-    far_low = along(up_low, 1, n_own)
-    far_high = along(down_high, -1, n_own)
-    for low, high, step in (
-        (up_low, up_high, last - 1), (down_low, down_high, 1 - last), (far_low, far_high, last)
-    ):
-        queries.append((len(arrays), len(arrays) + 1, step))
-        arrays += [low, high]
+    far_low = along(up[-1][: ROWS // 2], 1, n_own)
+    far_high = along(down[-1][ROWS // 2 :], -1, n_own)
+    queries.append((len(arrays), len(arrays) + 1, n_own // 2))
+    arrays += [far_low, far_high]
 
     held = {(0, 0): shard}
     keys = [(0, 0, 0, 0), (len(arrays), 0, 0, 1)]

time: 140 us -> 144 us (1.029)
  waiting for transfers between devices: 57.5 us -> 69.1 us
  starting transfers between devices: 42.1 us -> 35.4 us
    ppermute x10 -> x8, starting transfers between devices: 21.8 us -> 13 us  [along(): lax.ppermute(value, 'own', [(i, (i + step) % count) for i in range(count)])]
    ppermute x15, waiting for transfers between devices: 37.1 us -> 45.1 us  [in_plane(): return lax.ppermute(value, 'grp', plane_pairs(dx, dy, 0))]
    ppermute x10 -> x8, waiting for transfers between devices: 18.9 us -> 21.6 us  [along(): lax.ppermute(value, 'own', [(i, (i + step) % count) for i in range(count)])]
    ppermute x15, starting transfers between devices: 17.8 us -> 19.8 us  [in_plane(): return lax.ppermute(value, 'grp', plane_pairs(dx, dy, 0))]
  transfers between devices with their start and end apart: 41 -> 39, of which waited for: 18 -> 19; matrix products, arithmetic and copies ran while one was open for 1% -> 0% of each run, Pallas kernels for 0% -> 0%
where the time goes in v2:
time: 144 us; the launch traced here: 142 us
  waiting for transfers between devices  69.1 us (48%)
  starting transfers between devices  35.4 us (25%)
  Pallas kernels  19.8 us (14%)
  blocking collectives  13.8 us (10%)
  other arithmetic  2.12 us (1%)
  local copies, waits for them, and re-layouts  1.54 us (1%)
    ppermute x15, waiting for transfers between devices, in_plane(): return lax.ppermute(value, 'grp', plane_pairs(dx, dy, 0))  45.1 us
    ppermute x8, waiting for transfers between devices, along(): lax.ppermute(value, 'own', [(i, (i + step) % count) for i in range(count)])  21.6 us
    pallas_call x1, Pallas kernels, compare(): pl.pallas_call(functools.partial(compare_kernel, queries, keys), out_shap...  19.8 us
    ppermute x15, starting transfers between devices, in_plane(): return lax.ppermute(value, 'grp', plane_pairs(dx, dy, 0))  19.8 us
    all_to_all x1, blocking collectives, search(): lax.all_to_all(best, 'own', split_axis=0, concat_axis=0, tiled=True)  13.8 us
    ppermute x8, starting transfers between devices, along(): lax.ppermute(value, 'own', [(i, (i + step) % count) for i in range(count)])  13 us
  transfers between devices with their start and end apart: 39, of which 19 were waited for; matrix products, arithmetic and copies ran while one was open for 0% of the time, Pallas kernels for 0%

profile of v2, /device:TPU:32, one launch (start us, length us, event | category | flops | bytes accessed | tf_op | source)
XLA Modules:
  0.0 142.2 jit_solution(14017037652330798100)
XLA Ops:
  0.0 1.3 fusion
  1.3 0.2 fusion.1
  1.5 0.5 copy-done.32
  2.3 3.1 %collective-permute-start.15 = (bf16[264,1024]{1,0:T(8,128)(2,1)S(1)}, bf16[264,1024]{1,0:T(8,128)(2,1)S(1)}, u32[]{:S(2)}, u32[]{:S(2)}) collective-permute-start(bf16[264,1024]{1,0:T(8,128)(2,1)S(1)} %pad_maximum_fusion.refs_0_), channel_id=1, source_target_pairs={{0,192},{8,200},{16,208},{24,216},{32,224},{40,232},{48,240},{56,2... | collective-permute-start | bytes 1622024 | tf_op jit(solution)/shard_map/ppermute | solution.py:54
  5.4 1.5 %collective-permute-start.9 = (bf16[264,1024]{1,0:T(8,128)(2,1)S(1)}, bf16[264,1024]{1,0:T(8,128)(2,1)S(1)}, u32[]{:S(2)}, u32[]{:S(2)}) collective-permute-start(bf16[264,1024]{1,0:T(8,128)(2,1)S(1)} %pad_maximum_fusion.refs_0_), channel_id=1, source_target_pairs={{0,16},{8,24},{16,32},{24,40},{32,48},{40,56},{48,0},{56,8},{64,80... | collective-permute-start | bytes 1622024 | tf_op jit(solution)/shard_map/ppermute | solution.py:54
  6.9 1.7 %collective-permute-start.11 = (bf16[264,1024]{1,0:T(8,128)(2,1)S(1)}, bf16[264,1024]{1,0:T(8,128)(2,1)S(1)}, u32[]{:S(2)}, u32[]{:S(2)}) collective-permute-start(bf16[264,1024]{1,0:T(8,128)(2,1)S(1)} %pad_maximum_fusion.refs_0_), channel_id=1, source_target_pairs={{0,48},{8,56},{16,0},{24,8},{32,16},{40,24},{48,32},{56,40},{64,11... | collective-permute-start | bytes 1622024 | tf_op jit(solution)/shard_map/ppermute | solution.py:54
  8.6 0.8 collective-permute-start.1
  9.4 7.5 %collective-permute-done.15.refs_16_ = bf16[264,1024]{1,0:T(8,128)(2,1)S(1)} collective-permute-done((bf16[264,1024]{1,0:T(8,128)(2,1)S(1)}, bf16[264,1024]{1,0:T(8,128)(2,1)S(1)}, u32[]{:S(2)}, u32[]{:S(2)}) %collective-permute-start.15) | collective-permute-done | bytes 540704 | tf_op jit(solution)/shard_map/ppermute | solution.py:54
  16.9 1.9 %collective-permute-start = (bf16[264,1024]{1,0:T(8,128)(2,1)S(1)}, bf16[264,1024]{1,0:T(8,128)(2,1)S(1)}, u32[]{:S(2)}, u32[]{:S(2)}) collective-permute-start(bf16[264,1024]{1,0:T(8,128)(2,1)S(1)} %pad_maximum_fusion.refs_0_), channel_id=1, source_target_pairs={{0,1},{1,2},{2,3},{3,4},{4,5},{5,6},{6,7},{7,0},{8,9},{9,10},{10,1... | collective-permute-start | bytes 1622024 | tf_op jit(solution)/shard_map/ppermute | solution.py:62
  18.8 1.5 %collective-permute-done.9.refs_10_ = bf16[264,1024]{1,0:T(8,128)(2,1)S(1)} collective-permute-done((bf16[264,1024]{1,0:T(8,128)(2,1)S(1)}, bf16[264,1024]{1,0:T(8,128)(2,1)S(1)}, u32[]{:S(2)}, u32[]{:S(2)}) %collective-permute-start.9) | collective-permute-done | bytes 540704 | tf_op jit(solution)/shard_map/ppermute | solution.py:54
  20.3 1.2 collective-permute-done.13.refs_14_
  21.5 1.7 %collective-permute-start.19 = (bf16[264,1024]{1,0:T(8,128)(2,1)S(1)}, bf16[264,1024]{1,0:T(8,128)(2,1)S(1)}, u32[]{:S(2)}, u32[]{:S(2)}) collective-permute-start(bf16[264,1024]{1,0:T(8,128)(2,1)S(1)} %collective-permute-done.15.refs_16_), channel_id=1, source_target_pairs={{0,48},{8,56},{16,0},{24,8},{32,16},{40,24},{48,32},{56,40},{64,11... | collective-permute-start | bytes 1622024 | tf_op jit(solution)/shard_map/ppermute | solution.py:54
  23.3 2.1 %collective-permute-start.23 = (bf16[264,1024]{1,0:T(8,128)(2,1)S(1)}, bf16[264,1024]{1,0:T(8,128)(2,1)S(1)}, u32[]{:S(2)}, u32[]{:S(2)}) collective-permute-start(bf16[264,1024]{1,0:T(8,128)(2,1)S(1)} %collective-permute-done.9.refs_10_), channel_id=1, source_target_pairs={{0,192},{8,200},{16,208},{24,216},{32,224},{40,232},{48,240},{56,2... | collective-permute-start | bytes 1622024 | tf_op jit(solution)/shard_map/ppermute | solution.py:54
  25.4 4.7 %collective-permute-done.refs_1_ = bf16[264,1024]{1,0:T(8,128)(2,1)S(1)} collective-permute-done((bf16[264,1024]{1,0:T(8,128)(2,1)S(1)}, bf16[264,1024]{1,0:T(8,128)(2,1)S(1)}, u32[]{:S(2)}, u32[]{:S(2)}) %collective-permute-start) | collective-permute-done | bytes 540704 | tf_op jit(solution)/shard_map/ppermute | solution.py:62
  30.1 1.0 collective-permute-start.21
  31.1 1.5 %collective-permute-start.25 = (bf16[264,1024]{1,0:T(8,128)(2,1)S(1)}, bf16[264,1024]{1,0:T(8,128)(2,1)S(1)}, u32[]{:S(2)}, u32[]{:S(2)}) collective-permute-start(bf16[264,1024]{1,0:T(8,128)(2,1)S(1)} %collective-permute-done.9.refs_10_), channel_id=1, source_target_pairs={{0,16},{8,24},{16,32},{24,40},{32,48},{40,56},{48,0},{56,8},{64,80... | collective-permute-start | bytes 1622024 | tf_op jit(solution)/shard_map/ppermute | solution.py:54
  32.6 2.4 %collective-permute-done.19.refs_20_ = bf16[264,1024]{1,0:T(8,128)(2,1)S(1)} collective-permute-done((bf16[264,1024]{1,0:T(8,128)(2,1)S(1)}, bf16[264,1024]{1,0:T(8,128)(2,1)S(1)}, u32[]{:S(2)}, u32[]{:S(2)}) %collective-permute-start.19) | collective-permute-done | bytes 540704 | tf_op jit(solution)/shard_map/ppermute | solution.py:54
  35.0 2.2 %collective-permute-done.23.refs_24_ = bf16[264,1024]{1,0:T(8,128)(2,1)S(1)} collective-permute-done((bf16[264,1024]{1,0:T(8,128)(2,1)S(1)}, bf16[264,1024]{1,0:T(8,128)(2,1)S(1)}, u32[]{:S(2)}, u32[]{:S(2)}) %collective-permute-start.23) | collective-permute-done | bytes 540704 | tf_op jit(solution)/shard_map/ppermute | solution.py:54
  37.2 1.2 collective-permute-start.3
  38.4 3.3 %collective-permute-done.17.refs_18_ = bf16[264,1024]{1,0:T(8,128)(2,1)S(1)} collective-permute-done((bf16[264,1024]{1,0:T(8,128)(2,1)S(1)}, bf16[264,1024]{1,0:T(8,128)(2,1)S(1)}, u32[]{:S(2)}, u32[]{:S(2)}) %collective-permute-start.17) | collective-permute-done | bytes 540704 | tf_op jit(solution)/shard_map/ppermute | solution.py:54
  41.8 1.9 %collective-permute-start.2 = (bf16[264,1024]{1,0:T(8,128)(2,1)S(1)}, bf16[264,1024]{1,0:T(8,128)(2,1)S(1)}, u32[]{:S(2)}, u32[]{:S(2)}) collective-permute-start(bf16[264,1024]{1,0:T(8,128)(2,1)S(1)} %collective-permute-done.refs_1_), channel_id=1, source_target_pairs={{0,1},{1,2},{2,3},{3,4},{4,5},{5,6},{6,7},{7,0},{8,9},{9,10},{10,1... | collective-permute-start | bytes 1622024 | tf_op jit(solution)/shard_map/ppermute | solution.py:62
  43.7 3.2 %collective-permute-done.21.refs_22_ = bf16[264,1024]{1,0:T(8,128)(2,1)S(1)} collective-permute-done((bf16[264,1024]{1,0:T(8,128)(2,1)S(1)}, bf16[264,1024]{1,0:T(8,128)(2,1)S(1)}, u32[]{:S(2)}, u32[]{:S(2)}) %collective-permute-start.21) | collective-permute-done | bytes 540704 | tf_op jit(solution)/shard_map/ppermute | solution.py:54
  46.9 5.3 %collective-permute-done.25.refs_26_ = bf16[264,1024]{1,0:T(8,128)(2,1)S(1)} collective-permute-done((bf16[264,1024]{1,0:T(8,128)(2,1)S(1)}, bf16[264,1024]{1,0:T(8,128)(2,1)S(1)}, u32[]{:S(2)}, u32[]{:S(2)}) %collective-permute-start.25) | collective-permute-done | bytes 540704 | tf_op jit(solution)/shard_map/ppermute | solution.py:54
  52.2 3.7 %collective-permute-done.29.refs_30_ = bf16[264,1024]{1,0:T(8,128)(2,1)S(1)} collective-permute-done((bf16[264,1024]{1,0:T(8,128)(2,1)S(1)}, bf16[264,1024]{1,0:T(8,128)(2,1)S(1)}, u32[]{:S(2)}, u32[]{:S(2)}) %collective-permute-start.29) | collective-permute-done | bytes 540704 | tf_op jit(solution)/shard_map/ppermute | solution.py:54
  55.9 0.5 collective-permute-start.16
  56.4 2.8 %collective-permute-start.27 = (bf16[264,1024]{1,0:T(8,128)(2,1)S(1)}, bf16[264,1024]{1,0:T(8,128)(2,1)}, u32[]{:S(2)}, u32[]{:S(2)}) collective-permute-start(bf16[264,1024]{1,0:T(8,128)(2,1)S(1)} %collective-permute-done.19.refs_20_), channel_id=1, source_target_pairs={{0,48},{8,56},{16,0},{24,8},{32,16},{40,24},{48,32},{56,40},{64,11... | collective-permute-start | bytes 1622024 | tf_op jit(solution)/shard_map/ppermute | solution.py:54
  59.2 1.7 %collective-permute-start.31 = (bf16[264,1024]{1,0:T(8,128)(2,1)S(1)}, bf16[264,1024]{1,0:T(8,128)(2,1)}, u32[]{:S(2)}, u32[]{:S(2)}) collective-permute-start(bf16[264,1024]{1,0:T(8,128)(2,1)S(1)} %collective-permute-done.23.refs_24_), channel_id=1, source_target_pairs={{0,192},{8,200},{16,208},{24,216},{32,224},{40,232},{48,240},{56,2... | collective-permute-start | bytes 1622024 | tf_op jit(solution)/shard_map/ppermute | solution.py:54
  61.0 0.4 collective-permute-start.35
  61.4 9.6 %collective-permute-done.27.refs_28_ = bf16[264,1024]{1,0:T(8,128)(2,1)} collective-permute-done((bf16[264,1024]{1,0:T(8,128)(2,1)S(1)}, bf16[264,1024]{1,0:T(8,128)(2,1)}, u32[]{:S(2)}, u32[]{:S(2)}) %collective-permute-start.27) | collective-permute-done | bytes 540704 | tf_op jit(solution)/shard_map/ppermute | solution.py:54
  71.0 2.3 %collective-permute-done.31.refs_32_ = bf16[264,1024]{1,0:T(8,128)(2,1)} collective-permute-done((bf16[264,1024]{1,0:T(8,128)(2,1)S(1)}, bf16[264,1024]{1,0:T(8,128)(2,1)}, u32[]{:S(2)}, u32[]{:S(2)}) %collective-permute-start.31) | collective-permute-done | bytes 540704 | tf_op jit(solution)/shard_map/ppermute | solution.py:54
  73.3 2.7 %collective-permute-done.33.refs_34_ = bf16[264,1024]{1,0:T(8,128)(2,1)} collective-permute-done((bf16[264,1024]{1,0:T(8,128)(2,1)S(1)}, bf16[264,1024]{1,0:T(8,128)(2,1)}, u32[]{:S(2)}, u32[]{:S(2)}) %collective-permute-start.33) | collective-permute-done | bytes 540704 | tf_op jit(solution)/shard_map/ppermute | solution.py:54
  76.0 4.5 %collective-permute-start.5 = (bf16[264,1024]{1,0:T(8,128)(2,1)S(1)}, bf16[264,1024]{1,0:T(8,128)(2,1)S(1)}, u32[]{:S(2)}, u32[]{:S(2)}) collective-permute-start(bf16[264,1024]{1,0:T(8,128)(2,1)S(1)} %collective-permute-done.3.refs_4_), channel_id=1, source_target_pairs={{0,7},{1,0},{2,1},{3,2},{4,3},{5,4},{6,5},{7,6},{8,15},{9,8},{10,9... | collective-permute-start | bytes 1622024 | tf_op jit(solution)/shard_map/ppermute | solution.py:62
  80.6 0.5 collective-permute-start.26
  81.1 0.1 collective-permute-start.30
  81.2 9.6 %collective-permute-done.5.refs_6_ = bf16[264,1024]{1,0:T(8,128)(2,1)S(1)} collective-permute-done((bf16[264,1024]{1,0:T(8,128)(2,1)S(1)}, bf16[264,1024]{1,0:T(8,128)(2,1)S(1)}, u32[]{:S(2)}, u32[]{:S(2)}) %collective-permute-start.5) | collective-permute-done | bytes 540704 | tf_op jit(solution)/shard_map/ppermute | solution.py:62
  91.0 2.2 %collective-permute-start.37 = (bf16[264,1024]{1,0:T(8,128)(2,1)}, bf16[264,1024]{1,0:T(8,128)(2,1)}, u32[]{:S(2)}, u32[]{:S(2)}) collective-permute-start(bf16[264,1024]{1,0:T(8,128)(2,1)} %collective-permute-done.27.refs_28_), channel_id=1, source_target_pairs={{0,192},{8,200},{16,208},{24,216},{32,224},{40,232},{48,240},{56,2... | collective-permute-start | bytes 1622024 | tf_op jit(solution)/shard_map/ppermute | solution.py:54
  93.2 2.6 %collective-permute-start.7 = (bf16[136,1024]{1,0:T(8,128)(2,1)S(1)}, bf16[136,1024]{1,0:T(8,128)(2,1)S(1)}, u32[]{:S(2)}, u32[]{:S(2)}) collective-permute-start(bf16[136,1024]{1,0:T(8,128)(2,1)S(1)} %slice.9), channel_id=1, source_target_pairs={{0,7},{1,0},{2,1},{3,2},{4,3},{5,4},{6,5},{7,6},{8,15},{9,8},{10,9... | collective-permute-start | bytes 835592 | tf_op jit(solution)/shard_map/ppermute | solution.py:62
  96.0 0.3 collective-permute-start.28
  96.3 0.5 collective-permute-start.32
  96.8 7.3 %collective-permute-done.6.refs_7_ = bf16[128,1024]{1,0:T(8,128)(2,1)S(1)} collective-permute-done((bf16[128,1024]{1,0:T(8,128)(2,1)S(1)}, bf16[128,1024]{1,0:T(8,128)(2,1)S(1)}, u32[]{:S(2)}, u32[]{:S(2)}) %collective-permute-start.6) | collective-permute-done | bytes 262176 | tf_op jit(solution)/shard_map/ppermute | solution.py:62
  104.1 0.6 collective-permute-start.36
  104.8 0.6 pad_add_fusion.where_ref
  105.4 0.9 collective-permute-done.34.refs_35_
  106.3 0.8 collective-permute-done.36.refs_37_
  107.1 0.8 collective-permute-done.38.refs_39_
  107.9 19.8 %compare.36 = f32[8,1,256]{2,1,0:T(1,128)} custom-call(s32[2]{0:T(128)} %pad_add_fusion.where_ref, s32[32,32]{1,0:T(8,128)} %pattern_ref.1, bf16[264,1024]{1,0:T(8,128)(2,1)} %copy-done.1, bf16[264,1024]{1,0:T(8,128)(2,1)} %copy-done.10, bf16[264,1024]{1,0:T(8,128)(2,1)} %copy-done.9, bf16[264,1024]{1,0:T(8,128)(2,1)} %copy-done.19, ...), custom_call_target="tpu_custom_call" | custom-call | flops 8589934592 | bytes 20971520 | tf_op jit(solution)/shard_map/compare/pallas_call | solution.py:281
  127.7 13.8 %all_to_all.5 = f32[8,1,256]{2,1,0:T(1,128)S(1)} all-to-all(f32[8,1,256]{2,1,0:T(1,128)} %compare.36), channel_id=1, replica_groups=mesh['grp'=32,'own'=8] {'own'}, dimensions={0} | all-to-all | bytes 16384 | tf_op jit(solution)/shard_map/all_to_all | solution.py:351
  141.5 0.7 reshape.28
  (113 shorter events, 0.9 us)
Async XLA Ops:
  2.3 102.5 %copy-start.1 = (bf16[264,1024]{1,0:T(8,128)(2,1)}, bf16[264,1024]{1,0:T(8,128)(2,1)S(1)}, u32[]{:S(2)}) copy-start(bf16[264,1024]{1,0:T(8,128)(2,1)S(1)} %pad_maximum_fusion.refs_0_) | copy-start | bytes 1622020
  2.3 14.6 %collective-permute-start.15 = (bf16[264,1024]{1,0:T(8,128)(2,1)S(1)}, bf16[264,1024]{1,0:T(8,128)(2,1)S(1)}, u32[]{:S(2)}, u32[]{:S(2)}) collective-permute-start(bf16[264,1024]{1,0:T(8,128)(2,1)S(1)} %pad_maximum_fusion.refs_0_), channel_id=1, source_target_pairs={{0,192},{8,200},{16,208},{24,216},{32,224},{40,232},{48,240},{56,2... | collective-permute-start | bytes 1622024 | tf_op jit(solution)/shard_map/ppermute | solution.py:54
  5.4 14.9 %collective-permute-start.9 = (bf16[264,1024]{1,0:T(8,128)(2,1)S(1)}, bf16[264,1024]{1,0:T(8,128)(2,1)S(1)}, u32[]{:S(2)}, u32[]{:S(2)}) collective-permute-start(bf16[264,1024]{1,0:T(8,128)(2,1)S(1)} %pad_maximum_fusion.refs_0_), channel_id=1, source_target_pairs={{0,16},{8,24},{16,32},{24,40},{32,48},{40,56},{48,0},{56,8},{64,80... | collective-permute-start | bytes 1622024 | tf_op jit(solution)/shard_map/ppermute | solution.py:54
  6.9 14.7 %collective-permute-start.13 = (bf16[264,1024]{1,0:T(8,128)(2,1)S(1)}, bf16[264,1024]{1,0:T(8,128)(2,1)S(1)}, u32[]{:S(2)}, u32[]{:S(2)}) collective-permute-start(bf16[264,1024]{1,0:T(8,128)(2,1)S(1)} %pad_maximum_fusion.refs_0_), channel_id=1, source_target_pairs={{0,64},{8,72},{16,80},{24,88},{32,96},{40,104},{48,112},{56,120},{... | collective-permute-start | bytes 1622024 | tf_op jit(solution)/shard_map/ppermute | solution.py:54
  6.9 16.4 %collective-permute-start.11 = (bf16[264,1024]{1,0:T(8,128)(2,1)S(1)}, bf16[264,1024]{1,0:T(8,128)(2,1)S(1)}, u32[]{:S(2)}, u32[]{:S(2)}) collective-permute-start(bf16[264,1024]{1,0:T(8,128)(2,1)S(1)} %pad_maximum_fusion.refs_0_), channel_id=1, source_target_pairs={{0,48},{8,56},{16,0},{24,8},{32,16},{40,24},{48,32},{56,40},{64,11... | collective-permute-start | bytes 1622024 | tf_op jit(solution)/shard_map/ppermute | solution.py:54
  8.6 16.8 %collective-permute-start.1 = (bf16[264,1024]{1,0:T(8,128)(2,1)S(1)}, bf16[264,1024]{1,0:T(8,128)(2,1)S(1)}, u32[]{:S(2)}, u32[]{:S(2)}) collective-permute-start(bf16[264,1024]{1,0:T(8,128)(2,1)S(1)} %pad_maximum_fusion.refs_0_), channel_id=1, source_target_pairs={{0,7},{1,0},{2,1},{3,2},{4,3},{5,4},{6,5},{7,6},{8,15},{9,8},{10,9... | collective-permute-start | bytes 1622024 | tf_op jit(solution)/shard_map/ppermute | solution.py:62
  16.9 91.0 %copy-start.5 = (bf16[264,1024]{1,0:T(8,128)(2,1)}, bf16[264,1024]{1,0:T(8,128)(2,1)S(1)}, u32[]{:S(2)}) copy-start(bf16[264,1024]{1,0:T(8,128)(2,1)S(1)} %collective-permute-done.15.refs_16_) | copy-start | bytes 1622020
  16.9 13.2 %collective-permute-start = (bf16[264,1024]{1,0:T(8,128)(2,1)S(1)}, bf16[264,1024]{1,0:T(8,128)(2,1)S(1)}, u32[]{:S(2)}, u32[]{:S(2)}) collective-permute-start(bf16[264,1024]{1,0:T(8,128)(2,1)S(1)} %pad_maximum_fusion.refs_0_), channel_id=1, source_target_pairs={{0,1},{1,2},{2,3},{3,4},{4,5},{5,6},{6,7},{7,0},{8,9},{9,10},{10,1... | collective-permute-start | bytes 1622024 | tf_op jit(solution)/shard_map/ppermute | solution.py:62
  20.3 87.6 %copy-start.6 = (bf16[264,1024]{1,0:T(8,128)(2,1)}, bf16[264,1024]{1,0:T(8,128)(2,1)S(1)}, u32[]{:S(2)}) copy-start(bf16[264,1024]{1,0:T(8,128)(2,1)S(1)} %collective-permute-done.9.refs_10_) | copy-start | bytes 1622020
  20.3 10.8 %collective-permute-start.8 = (bf16[264,1024]{1,0:T(8,128)(2,1)S(1)}, bf16[264,1024]{1,0:T(8,128)(2,1)S(1)}, u32[]{:S(2)}, u32[]{:S(2)}) collective-permute-start(bf16[264,1024]{1,0:T(8,128)(2,1)S(1)} %pad_maximum_fusion.refs_0_), channel_id=1, source_target_pairs={{0,8},{8,0},{16,24},{24,16},{32,40},{40,32},{48,56},{56,48},{64,72... | collective-permute-start | bytes 1622024 | tf_op jit(solution)/shard_map/ppermute | solution.py:58
  21.5 86.4 %copy-start.7 = (bf16[264,1024]{1,0:T(8,128)(2,1)}, bf16[264,1024]{1,0:T(8,128)(2,1)S(1)}, u32[]{:S(2)}) copy-start(bf16[264,1024]{1,0:T(8,128)(2,1)S(1)} %collective-permute-done.13.refs_14_) | copy-start | bytes 1622020
  21.5 13.5 %collective-permute-start.19 = (bf16[264,1024]{1,0:T(8,128)(2,1)S(1)}, bf16[264,1024]{1,0:T(8,128)(2,1)S(1)}, u32[]{:S(2)}, u32[]{:S(2)}) collective-permute-start(bf16[264,1024]{1,0:T(8,128)(2,1)S(1)} %collective-permute-done.15.refs_16_), channel_id=1, source_target_pairs={{0,48},{8,56},{16,0},{24,8},{32,16},{40,24},{48,32},{56,40},{64,11... | collective-permute-start | bytes 1622024 | tf_op jit(solution)/shard_map/ppermute | solution.py:54
  23.3 67.6 %copy-start.8 = (bf16[264,1024]{1,0:T(8,128)(2,1)}, bf16[264,1024]{1,0:T(8,128)(2,1)S(1)}, u32[]{:S(2)}) copy-start(bf16[264,1024]{1,0:T(8,128)(2,1)S(1)} %collective-permute-done.11.refs_12_) | copy-start | bytes 1622020
  23.3 13.9 %collective-permute-start.23 = (bf16[264,1024]{1,0:T(8,128)(2,1)S(1)}, bf16[264,1024]{1,0:T(8,128)(2,1)S(1)}, u32[]{:S(2)}, u32[]{:S(2)}) collective-permute-start(bf16[264,1024]{1,0:T(8,128)(2,1)S(1)} %collective-permute-done.9.refs_10_), channel_id=1, source_target_pairs={{0,192},{8,200},{16,208},{24,216},{32,224},{40,232},{48,240},{56,2... | collective-permute-start | bytes 1622024 | tf_op jit(solution)/shard_map/ppermute | solution.py:54
  25.4 65.5 %copy-start.9 = (bf16[264,1024]{1,0:T(8,128)(2,1)}, bf16[264,1024]{1,0:T(8,128)(2,1)S(1)}, u32[]{:S(2)}) copy-start(bf16[264,1024]{1,0:T(8,128)(2,1)S(1)} %collective-permute-done.1.refs_2_) | copy-start | bytes 1622020
  25.4 16.4 %collective-permute-start.17 = (bf16[264,1024]{1,0:T(8,128)(2,1)S(1)}, bf16[264,1024]{1,0:T(8,128)(2,1)S(1)}, u32[]{:S(2)}, u32[]{:S(2)}) collective-permute-start(bf16[264,1024]{1,0:T(8,128)(2,1)S(1)} %collective-permute-done.13.refs_14_), channel_id=1, source_target_pairs={{0,16},{8,24},{16,32},{24,40},{32,48},{40,56},{48,0},{56,8},{64,80... | collective-permute-start | bytes 1622024 | tf_op jit(solution)/shard_map/ppermute | solution.py:54
  30.1 60.8 %copy-start.10 = (bf16[264,1024]{1,0:T(8,128)(2,1)}, bf16[264,1024]{1,0:T(8,128)(2,1)S(1)}, u32[]{:S(2)}) copy-start(bf16[264,1024]{1,0:T(8,128)(2,1)S(1)} %collective-permute-done.refs_1_) | copy-start | bytes 1622020
  30.1 16.8 %collective-permute-start.21 = (bf16[264,1024]{1,0:T(8,128)(2,1)S(1)}, bf16[264,1024]{1,0:T(8,128)(2,1)S(1)}, u32[]{:S(2)}, u32[]{:S(2)}) collective-permute-start(bf16[264,1024]{1,0:T(8,128)(2,1)S(1)} %collective-permute-done.11.refs_12_), channel_id=1, source_target_pairs={{0,64},{8,72},{16,80},{24,88},{32,96},{40,104},{48,112},{56,120},{... | collective-permute-start | bytes 1622024 | tf_op jit(solution)/shard_map/ppermute | solution.py:54
  31.1 59.8 %copy-start.11 = (bf16[264,1024]{1,0:T(8,128)(2,1)}, bf16[264,1024]{1,0:T(8,128)(2,1)S(1)}, u32[]{:S(2)}) copy-start(bf16[264,1024]{1,0:T(8,128)(2,1)S(1)} %collective-permute-done.8.refs_9_) | copy-start | bytes 1622020
  31.1 21.1 %collective-permute-start.25 = (bf16[264,1024]{1,0:T(8,128)(2,1)S(1)}, bf16[264,1024]{1,0:T(8,128)(2,1)S(1)}, u32[]{:S(2)}, u32[]{:S(2)}) collective-permute-start(bf16[264,1024]{1,0:T(8,128)(2,1)S(1)} %collective-permute-done.9.refs_10_), channel_id=1, source_target_pairs={{0,16},{8,24},{16,32},{24,40},{32,48},{40,56},{48,0},{56,8},{64,80... | collective-permute-start | bytes 1622024 | tf_op jit(solution)/shard_map/ppermute | solution.py:54
  35.0 20.9 %collective-permute-start.29 = (bf16[264,1024]{1,0:T(8,128)(2,1)S(1)}, bf16[264,1024]{1,0:T(8,128)(2,1)S(1)}, u32[]{:S(2)}, u32[]{:S(2)}) collective-permute-start(bf16[264,1024]{1,0:T(8,128)(2,1)S(1)} %collective-permute-done.13.refs_14_), channel_id=1, source_target_pairs={{0,64},{8,72},{16,80},{24,88},{32,96},{40,104},{48,112},{56,120},{... | collective-permute-start | bytes 1622024 | tf_op jit(solution)/shard_map/ppermute | solution.py:54
  37.2 18.7 %collective-permute-start.3 = (bf16[264,1024]{1,0:T(8,128)(2,1)S(1)}, bf16[264,1024]{1,0:T(8,128)(2,1)S(1)}, u32[]{:S(2)}, u32[]{:S(2)}) collective-permute-start(bf16[264,1024]{1,0:T(8,128)(2,1)S(1)} %collective-permute-done.1.refs_2_), channel_id=1, source_target_pairs={{0,7},{1,0},{2,1},{3,2},{4,3},{5,4},{6,5},{7,6},{8,15},{9,8},{10,9... | collective-permute-start | bytes 1622024 | tf_op jit(solution)/shard_map/ppermute | solution.py:62
  41.8 14.7 %collective-permute-start.2 = (bf16[264,1024]{1,0:T(8,128)(2,1)S(1)}, bf16[264,1024]{1,0:T(8,128)(2,1)S(1)}, u32[]{:S(2)}, u32[]{:S(2)}) collective-permute-start(bf16[264,1024]{1,0:T(8,128)(2,1)S(1)} %collective-permute-done.refs_1_), channel_id=1, source_target_pairs={{0,1},{1,2},{2,3},{3,4},{4,5},{5,6},{6,7},{7,0},{8,9},{9,10},{10,1... | collective-permute-start | bytes 1622024 | tf_op jit(solution)/shard_map/ppermute | solution.py:62
  46.9 57.2 %copy-start.15 = (bf16[264,1024]{1,0:T(8,128)(2,1)}, bf16[264,1024]{1,0:T(8,128)(2,1)S(1)}, u32[]{:S(2)}) copy-start(bf16[264,1024]{1,0:T(8,128)(2,1)S(1)} %collective-permute-done.21.refs_22_) | copy-start | bytes 1622020
  46.9 12.3 %collective-permute-start.10 = (bf16[264,1024]{1,0:T(8,128)(2,1)S(1)}, bf16[264,1024]{1,0:T(8,128)(2,1)S(1)}, u32[]{:S(2)}, u32[]{:S(2)}) collective-permute-start(bf16[264,1024]{1,0:T(8,128)(2,1)S(1)} %collective-permute-done.9.refs_10_), channel_id=1, source_target_pairs={{0,8},{8,0},{16,24},{24,16},{32,40},{40,32},{48,56},{56,48},{64,72... | collective-permute-start | bytes 1622024 | tf_op jit(solution)/shard_map/ppermute | solution.py:58
  52.2 8.7 %collective-permute-start.14 = (bf16[264,1024]{1,0:T(8,128)(2,1)S(1)}, bf16[264,1024]{1,0:T(8,128)(2,1)S(1)}, u32[]{:S(2)}, u32[]{:S(2)}) collective-permute-start(bf16[264,1024]{1,0:T(8,128)(2,1)S(1)} %collective-permute-done.13.refs_14_), channel_id=1, source_target_pairs={{0,8},{8,0},{16,24},{24,16},{32,40},{40,32},{48,56},{56,48},{64,72... | collective-permute-start | bytes 1622024 | tf_op jit(solution)/shard_map/ppermute | solution.py:58
  55.9 5.0 %collective-permute-start.12 = (bf16[264,1024]{1,0:T(8,128)(2,1)S(1)}, bf16[264,1024]{1,0:T(8,128)(2,1)S(1)}, u32[]{:S(2)}, u32[]{:S(2)}) collective-permute-start(bf16[264,1024]{1,0:T(8,128)(2,1)S(1)} %collective-permute-done.11.refs_12_), channel_id=1, source_target_pairs={{0,8},{8,0},{16,24},{24,16},{32,40},{40,32},{48,56},{56,48},{64,72... | collective-permute-start | bytes 1622024 | tf_op jit(solution)/shard_map/ppermute | solution.py:58
  55.9 5.4 %collective-permute-start.16 = (bf16[264,1024]{1,0:T(8,128)(2,1)S(1)}, bf16[264,1024]{1,0:T(8,128)(2,1)S(1)}, u32[]{:S(2)}, u32[]{:S(2)}) collective-permute-start(bf16[264,1024]{1,0:T(8,128)(2,1)S(1)} %collective-permute-done.15.refs_16_), channel_id=1, source_target_pairs={{0,8},{8,0},{16,24},{24,16},{32,40},{40,32},{48,56},{56,48},{64,72... | collective-permute-start | bytes 1622024 | tf_op jit(solution)/shard_map/ppermute | solution.py:58
  56.4 14.6 %collective-permute-start.27 = (bf16[264,1024]{1,0:T(8,128)(2,1)S(1)}, bf16[264,1024]{1,0:T(8,128)(2,1)}, u32[]{:S(2)}, u32[]{:S(2)}) collective-permute-start(bf16[264,1024]{1,0:T(8,128)(2,1)S(1)} %collective-permute-done.19.refs_20_), channel_id=1, source_target_pairs={{0,48},{8,56},{16,0},{24,8},{32,16},{40,24},{48,32},{56,40},{64,11... | collective-permute-start | bytes 1622024 | tf_op jit(solution)/shard_map/ppermute | solution.py:54
  59.2 14.1 %collective-permute-start.31 = (bf16[264,1024]{1,0:T(8,128)(2,1)S(1)}, bf16[264,1024]{1,0:T(8,128)(2,1)}, u32[]{:S(2)}, u32[]{:S(2)}) collective-permute-start(bf16[264,1024]{1,0:T(8,128)(2,1)S(1)} %collective-permute-done.23.refs_24_), channel_id=1, source_target_pairs={{0,192},{8,200},{16,208},{24,216},{32,224},{40,232},{48,240},{56,2... | collective-permute-start | bytes 1622024 | tf_op jit(solution)/shard_map/ppermute | solution.py:54
  61.0 15.0 %collective-permute-start.33 = (bf16[264,1024]{1,0:T(8,128)(2,1)S(1)}, bf16[264,1024]{1,0:T(8,128)(2,1)}, u32[]{:S(2)}, u32[]{:S(2)}) collective-permute-start(bf16[264,1024]{1,0:T(8,128)(2,1)S(1)} %collective-permute-done.17.refs_18_), channel_id=1, source_target_pairs={{0,16},{8,24},{16,32},{24,40},{32,48},{40,56},{48,0},{56,8},{64,80... | collective-permute-start | bytes 1622024 | tf_op jit(solution)/shard_map/ppermute | solution.py:54
  61.0 19.5 %collective-permute-start.35 = (bf16[264,1024]{1,0:T(8,128)(2,1)S(1)}, bf16[264,1024]{1,0:T(8,128)(2,1)}, u32[]{:S(2)}, u32[]{:S(2)}) collective-permute-start(bf16[264,1024]{1,0:T(8,128)(2,1)S(1)} %collective-permute-done.21.refs_22_), channel_id=1, source_target_pairs={{0,64},{8,72},{16,80},{24,88},{32,96},{40,104},{48,112},{56,120},{... | collective-permute-start | bytes 1622024 | tf_op jit(solution)/shard_map/ppermute | solution.py:54
  61.3 19.2 %collective-permute-start.18 = (bf16[264,1024]{1,0:T(8,128)(2,1)S(1)}, bf16[264,1024]{1,0:T(8,128)(2,1)S(1)}, u32[]{:S(2)}, u32[]{:S(2)}) collective-permute-start(bf16[264,1024]{1,0:T(8,128)(2,1)S(1)} %collective-permute-done.17.refs_18_), channel_id=1, source_target_pairs={{0,8},{8,0},{16,24},{24,16},{32,40},{40,32},{48,56},{56,48},{64,72... | collective-permute-start | bytes 1622024 | tf_op jit(solution)/shard_map/ppermute | solution.py:58
  71.0 9.6 %collective-permute-start.24 = (bf16[264,1024]{1,0:T(8,128)(2,1)S(1)}, bf16[264,1024]{1,0:T(8,128)(2,1)S(1)}, u32[]{:S(2)}, u32[]{:S(2)}) collective-permute-start(bf16[264,1024]{1,0:T(8,128)(2,1)S(1)} %collective-permute-done.23.refs_24_), channel_id=1, source_target_pairs={{0,8},{8,0},{16,24},{24,16},{32,40},{40,32},{48,56},{56,48},{64,72... | collective-permute-start | bytes 1622024 | tf_op jit(solution)/shard_map/ppermute | solution.py:58
  73.3 7.8 %collective-permute-start.20 = (bf16[264,1024]{1,0:T(8,128)(2,1)S(1)}, bf16[264,1024]{1,0:T(8,128)(2,1)S(1)}, u32[]{:S(2)}, u32[]{:S(2)}) collective-permute-start(bf16[264,1024]{1,0:T(8,128)(2,1)S(1)} %collective-permute-done.19.refs_20_), channel_id=1, source_target_pairs={{0,8},{8,0},{16,24},{24,16},{32,40},{40,32},{48,56},{56,48},{64,72... | collective-permute-start | bytes 1622024 | tf_op jit(solution)/shard_map/ppermute | solution.py:58
  76.0 14.9 %collective-permute-start.5 = (bf16[264,1024]{1,0:T(8,128)(2,1)S(1)}, bf16[264,1024]{1,0:T(8,128)(2,1)S(1)}, u32[]{:S(2)}, u32[]{:S(2)}) collective-permute-start(bf16[264,1024]{1,0:T(8,128)(2,1)S(1)} %collective-permute-done.3.refs_4_), channel_id=1, source_target_pairs={{0,7},{1,0},{2,1},{3,2},{4,3},{5,4},{6,5},{7,6},{8,15},{9,8},{10,9... | collective-permute-start | bytes 1622024 | tf_op jit(solution)/shard_map/ppermute | solution.py:62
  80.5 12.7 %collective-permute-start.4 = (bf16[264,1024]{1,0:T(8,128)(2,1)S(1)}, bf16[264,1024]{1,0:T(8,128)(2,1)S(1)}, u32[]{:S(2)}, u32[]{:S(2)}) collective-permute-start(bf16[264,1024]{1,0:T(8,128)(2,1)S(1)} %collective-permute-done.2.refs_3_), channel_id=1, source_target_pairs={{0,1},{1,2},{2,3},{3,4},{4,5},{5,6},{6,7},{7,0},{8,9},{9,10},{10,1... | collective-permute-start | bytes 1622024 | tf_op jit(solution)/shard_map/ppermute | solution.py:62
  80.5 15.3 %collective-permute-start.22 = (bf16[264,1024]{1,0:T(8,128)(2,1)S(1)}, bf16[264,1024]{1,0:T(8,128)(2,1)S(1)}, u32[]{:S(2)}, u32[]{:S(2)}) collective-permute-start(bf16[264,1024]{1,0:T(8,128)(2,1)S(1)} %collective-permute-done.21.refs_22_), channel_id=1, source_target_pairs={{0,8},{8,0},{16,24},{24,16},{32,40},{40,32},{48,56},{56,48},{64,72... | collective-permute-start | bytes 1622024 | tf_op jit(solution)/shard_map/ppermute | solution.py:58
  80.6 15.3 %collective-permute-start.26 = (bf16[264,1024]{1,0:T(8,128)(2,1)S(1)}, bf16[264,1024]{1,0:T(8,128)(2,1)S(1)}, u32[]{:S(2)}, u32[]{:S(2)}) collective-permute-start(bf16[264,1024]{1,0:T(8,128)(2,1)S(1)} %collective-permute-done.25.refs_26_), channel_id=1, source_target_pairs={{0,8},{8,0},{16,24},{24,16},{32,40},{40,32},{48,56},{56,48},{64,72... | collective-permute-start | bytes 1622024 | tf_op jit(solution)/shard_map/ppermute | solution.py:58
  81.1 15.2 %collective-permute-start.30 = (bf16[264,1024]{1,0:T(8,128)(2,1)S(1)}, bf16[264,1024]{1,0:T(8,128)(2,1)S(1)}, u32[]{:S(2)}, u32[]{:S(2)}) collective-permute-start(bf16[264,1024]{1,0:T(8,128)(2,1)S(1)} %collective-permute-done.29.refs_30_), channel_id=1, source_target_pairs={{0,8},{8,0},{16,24},{24,16},{32,40},{40,32},{48,56},{56,48},{64,72... | collective-permute-start | bytes 1622024 | tf_op jit(solution)/shard_map/ppermute | solution.py:58
  91.0 13.8 %collective-permute-start.37 = (bf16[264,1024]{1,0:T(8,128)(2,1)}, bf16[264,1024]{1,0:T(8,128)(2,1)}, u32[]{:S(2)}, u32[]{:S(2)}) collective-permute-start(bf16[264,1024]{1,0:T(8,128)(2,1)} %collective-permute-done.27.refs_28_), channel_id=1, source_target_pairs={{0,192},{8,200},{16,208},{24,216},{32,224},{40,232},{48,240},{56,2... | collective-permute-start | bytes 1622024 | tf_op jit(solution)/shard_map/ppermute | solution.py:54
  93.2 10.8 %collective-permute-start.7 = (bf16[136,1024]{1,0:T(8,128)(2,1)S(1)}, bf16[136,1024]{1,0:T(8,128)(2,1)S(1)}, u32[]{:S(2)}, u32[]{:S(2)}) collective-permute-start(bf16[136,1024]{1,0:T(8,128)(2,1)S(1)} %slice.9), channel_id=1, source_target_pairs={{0,7},{1,0},{2,1},{3,2},{4,3},{5,4},{6,5},{7,6},{8,15},{9,8},{10,9... | collective-permute-start | bytes 835592 | tf_op jit(solution)/shard_map/ppermute | solution.py:62
  95.8 8.2 %collective-permute-start.6 = (bf16[128,1024]{1,0:T(8,128)(2,1)S(1)}, bf16[128,1024]{1,0:T(8,128)(2,1)S(1)}, u32[]{:S(2)}, u32[]{:S(2)}) collective-permute-start(bf16[128,1024]{1,0:T(8,128)(2,1)S(1)} %slice.8), channel_id=1, source_target_pairs={{0,1},{1,2},{2,3},{3,4},{4,5},{5,6},{6,7},{7,0},{8,9},{9,10},{10,1... | collective-permute-start | bytes 786440 | tf_op jit(solution)/shard_map/ppermute | solution.py:62
  96.0 9.5 %collective-permute-start.28 = (bf16[264,1024]{1,0:T(8,128)(2,1)}, bf16[264,1024]{1,0:T(8,128)(2,1)}, u32[]{:S(2)}, u32[]{:S(2)}) collective-permute-start(bf16[264,1024]{1,0:T(8,128)(2,1)} %collective-permute-done.27.refs_28_), channel_id=1, source_target_pairs={{0,8},{8,0},{16,24},{24,16},{32,40},{40,32},{48,56},{56,48},{64,72... | collective-permute-start | bytes 1622024 | tf_op jit(solution)/shard_map/ppermute | solution.py:58
  96.3 9.1 %collective-permute-start.32 = (bf16[264,1024]{1,0:T(8,128)(2,1)}, bf16[264,1024]{1,0:T(8,128)(2,1)}, u32[]{:S(2)}, u32[]{:S(2)}) collective-permute-start(bf16[264,1024]{1,0:T(8,128)(2,1)} %collective-permute-done.31.refs_32_), channel_id=1, source_target_pairs={{0,8},{8,0},{16,24},{24,16},{32,40},{40,32},{48,56},{56,48},{64,72... | collective-permute-start | bytes 1622024 | tf_op jit(solution)/shard_map/ppermute | solution.py:58
  104.1 2.3 %collective-permute-start.34 = (bf16[264,1024]{1,0:T(8,128)(2,1)}, bf16[264,1024]{1,0:T(8,128)(2,1)}, u32[]{:S(2)}, u32[]{:S(2)}) collective-permute-start(bf16[264,1024]{1,0:T(8,128)(2,1)} %collective-permute-done.33.refs_34_), channel_id=1, source_target_pairs={{0,8},{8,0},{16,24},{24,16},{32,40},{40,32},{48,56},{56,48},{64,72... | collective-permute-start | bytes 1622024 | tf_op jit(solution)/shard_map/ppermute | solution.py:58
  104.1 3.0 %collective-permute-start.36 = (bf16[264,1024]{1,0:T(8,128)(2,1)}, bf16[264,1024]{1,0:T(8,128)(2,1)}, u32[]{:S(2)}, u32[]{:S(2)}) collective-permute-start(bf16[264,1024]{1,0:T(8,128)(2,1)} %collective-permute-done.35.refs_36_), channel_id=1, source_target_pairs={{0,8},{8,0},{16,24},{24,16},{32,40},{40,32},{48,56},{56,48},{64,72... | collective-permute-start | bytes 1622024 | tf_op jit(solution)/shard_map/ppermute | solution.py:58
  104.8 3.1 %collective-permute-start.38 = (bf16[264,1024]{1,0:T(8,128)(2,1)}, bf16[264,1024]{1,0:T(8,128)(2,1)}, u32[]{:S(2)}, u32[]{:S(2)}) collective-permute-start(bf16[264,1024]{1,0:T(8,128)(2,1)} %collective-permute-done.37.refs_38_), channel_id=1, source_target_pairs={{0,8},{8,0},{16,24},{24,16},{32,40},{40,32},{48,56},{56,48},{64,72... | collective-permute-start | bytes 1622024 | tf_op jit(solution)/shard_map/ppermute | solution.py:58
  (24 other events, 557.5 us)
